TPU v7x, 32 devices: a whole 2x2x4 slice. The times are simulated.
32 devices in a mesh: dp: 2 (over y), head: 4 (over x, core), col: 4 (over z).
Axes of the slice: x: 2, y: 2, z: 4, core: 2. Of those that a mesh axis runs over, the one named last changes fastest.
Arguments:
- encoder_token_ids: int32 [8, 1024], P('dp', ('head', 'col')), may hold values from 0 to 32127
- decoder_token_ids: int32 [8, 1024], P('dp', ('head', 'col')), may hold values from 0 to 32127
- target_token_ids: int32 [8, 1024], P('dp', ('head', 'col')), may hold values from 0 to 32127
- target_count_mask: int32 [8, 1024], P('dp', ('head', 'col')), may hold values from 0 to 1, as said below
- encoder_document_length: int32 [8, 4], P('dp'), may hold values from 1 to 512, 1024 in all within a row
- decoder_document_length: int32 [8, 4], P('dp'), may hold values from 1 to 512, 1024 in all within a row
- embedding: bfloat16 [32128, 768], P('col'), may hold values from -6 to 6
- attention_projection_weight: bfloat16 [3, 3, 768, 768], replicated, may hold values from -0.21875 to 0.21875
- attention_output_weight: bfloat16 [3, 768, 768], replicated, may hold values from -1.75 to 1.75
- feedforward_weight: bfloat16 [2, 2, 3072, 768], P(None, None, 'col'), may hold values from -0.21875 to 0.21875
- norm_gain_rows: float32 [7, 768], replicated, may hold values from 0.5 to 1.5
- earlier_down_weight: bfloat16 [6, 14, 8, 768], replicated, may hold values from -0.21875 to 0.21875
- adapter_down_weight: float32 [6, 8, 768], replicated, may hold values from -0.21875 to 0.21875
- adapter_up_weight: float32 [6, 8, 768], replicated, may hold values from -1 to 1
- down_first_moment: float32 [6, 8, 768], replicated, may hold values from -0.0546875 to 0.0546875
- down_second_moment: float32 [6, 8, 768], replicated, may hold values from 1.0986328e-06 to 4.394531e-06
- up_first_moment: float32 [6, 8, 768], replicated, may hold values from -0.015625 to 0.015625
- up_second_moment: float32 [6, 8, 768], replicated, may hold values from 1.2207032e-07 to 4.882813e-07
- optimizer_step_count: int32 [1], replicated, may hold values from 2 to 20
Outputs:
- loss_scalar: float32 [], replicated
- updated_down_weight: float32 [6, 8, 768], replicated
- down_first_updated: float32 [6, 8, 768], replicated
- down_second_updated: float32 [6, 8, 768], replicated
- updated_up_weight: float32 [6, 8, 768], replicated
- up_first_updated: float32 [6, 8, 768], replicated
- up_second_updated: float32 [6, 8, 768], replicated
Inputs may be any that keep to these rules, and one draw needn't show every extreme that they name: `encoder_document_length`: the 4 lengths of a row sum to 1024; the longest is 512. `decoder_document_length`: the 4 lengths of a row sum to 1024; the longest is 512. `target_count_mask`: the last position of every row is 1.
All inputs are finite; a program needn't handle non-finite values.
Results may differ from a plain program's by a relative error of at most 0.0027.
The roundings to bfloat16 on the way count: a program that leaves them out, or rounds other values in their place, can miss the bound.
Values may be sent and summed in bfloat16 or wider, within the bound.
No kernel may reach another device: no remote copies, remote signals or barrier semaphores. Data moves between devices by JAX's collectives and lax.ppermute only.
A program may use at most 192 MiB of HBM per device.

v0:
```python
import jax
import jax.numpy as jnp
from jax import lax
from jax.sharding import PartitionSpec as P

MODEL_DIMENSION = 768
HEAD_DIM = 64
ADAPTER_RANK = 8
LEN = 1024


ADAPTER_SCALE = 2.0
ORTH_WEIGHT = 0.2
BASE_NORM_WEIGHT = 0.02
DOWN_STEP_RATE = 0.05
UP_STEP_RATE = 0.2
BETA_ONE = 0.9
BETA_TWO = 0.999
ADAM_EPS = 1e-08
DECAY = 0.01
NEG_FILL = -1e30


def joined(x, axis, combine):
    everything = jax.tree.map(lambda part: lax.all_gather(part, axis), x)
    initial = jax.tree.map(lambda part: part[0], everything)

    def step(k, so_far):
        return combine(so_far, jax.tree.map(lambda part: part[k], everything))

    return lax.fori_loop(1, lax.axis_size(axis), step, initial)


def rms_norm(values, gain_row):
    return values * lax.rsqrt(jnp.mean(values * values, axis=-1, keepdims=True) + 1e-06) * gain_row


def norm_back(values, gain_row, grad_out, scale_by):
    primal, backward_function = jax.vjp(
        lambda inner_vals: rms_norm(inner_vals, gain_row) * scale_by, values
    )
    return backward_function(grad_out)[0]


def segment_of(lengths, length_total):
    bounds = jnp.cumsum(lengths, dtype=jnp.int32)
    places = jnp.arange(length_total, dtype=jnp.int32)
    return jnp.sum(
        (places[:, None] >= bounds[None, :-1]).astype(jnp.int32), axis=1, dtype=jnp.int32
    )


def col_rows(rows_low):
    return lax.all_gather(rows_low, "col", axis=0, tiled=True)


def col_sums(terms):
    return lax.psum_scatter(terms, "col", scatter_dimension=0, tiled=True)


def score_block(q_block, key_rows, seg_block, seg_key, start_at, causal):
    scores = jnp.einsum(
        "qhd,khd->hqk", q_block, key_rows, preferred_element_type=jnp.float32
    ) * HEAD_DIM ** (-0.5)
    allowed = seg_block[:, None] == seg_key[None, :]
    if causal:
        query_at = start_at + jnp.arange(q_block.shape[0], dtype=jnp.int32)
        key_at = jnp.arange(seg_key.shape[0], dtype=jnp.int32)
        allowed = allowed & (key_at[None, :] <= query_at[:, None])
    return jnp.where(allowed[None], scores, NEG_FILL)


def attend_forward(queries, key_rows, value_rows, seg_query, seg_key, causal):
    length_q, heads_here, head_width = queries.shape
    block_rows = min(512, length_q)
    blocks = length_q // block_rows

    def one_block(members):
        q_block, seg_block, start_at = members
        scores = score_block(q_block, key_rows, seg_block, seg_key, start_at, causal)
        row_top = jnp.max(scores, axis=2, keepdims=True)
        exponent = jnp.exp(scores - row_top)
        row_total = jnp.sum(exponent, axis=2, keepdims=True)
        probs_low = (exponent / row_total).astype(jnp.bfloat16)
        mixed_heads = jnp.einsum(
            "hqk,khd->qhd", probs_low, value_rows, preferred_element_type=jnp.float32
        )
        return (mixed_heads.astype(jnp.bfloat16), row_top, row_total)

    starts = jnp.arange(blocks, dtype=jnp.int32) * block_rows
    mixed_heads, row_tops, row_sums = lax.map(
        one_block,
        (
            queries.reshape(blocks, block_rows, heads_here, head_width),
            seg_query.reshape(blocks, block_rows),
            starts,
        ),
    )
    return (mixed_heads.reshape(length_q, heads_here, head_width), row_tops, row_sums)


def attend_backward(
    queries, key_rows, value_rows, seg_query, seg_key, causal, row_tops, row_sums, grad_mixed
):
    length_q, heads_here, head_width = queries.shape
    block_rows = min(512, length_q)
    blocks = length_q // block_rows
    score_scale = HEAD_DIM ** (-0.5)

    def one_block(carried, members):
        grad_keys, grad_values = carried
        q_block, seg_block, start_at, top_block, total_block, grad_block = members
        scores = score_block(q_block, key_rows, seg_block, seg_key, start_at, causal)
        probs_f = jnp.exp(scores - top_block) / total_block
        grad_probs = jnp.einsum(
            "qhd,khd->hqk", grad_block, value_rows, preferred_element_type=jnp.float32
        )
        inner_sum = jnp.sum(grad_probs * probs_f, axis=2, keepdims=True)
        grad_scores = (probs_f * (grad_probs - inner_sum)).astype(jnp.bfloat16)
        grad_q = (
            jnp.einsum("hqk,khd->qhd", grad_scores, key_rows, preferred_element_type=jnp.float32)
            * score_scale
        )
        grad_keys = (
            grad_keys
            + jnp.einsum("hqk,qhd->khd", grad_scores, q_block, preferred_element_type=jnp.float32)
            * score_scale
        )
        grad_values = grad_values + jnp.einsum(
            "hqk,qhd->khd",
            probs_f.astype(jnp.bfloat16),
            grad_block,
            preferred_element_type=jnp.float32,
        )
        return ((grad_keys, grad_values), grad_q)

    empty_kv = jnp.zeros(key_rows.shape, jnp.float32)
    starts = jnp.arange(blocks, dtype=jnp.int32) * block_rows
    members = (
        queries.reshape(blocks, block_rows, heads_here, head_width),
        seg_query.reshape(blocks, block_rows),
        starts,
        row_tops,
        row_sums,
        grad_mixed.reshape(blocks, block_rows, heads_here, head_width),
    )
    (grad_keys, grad_values), grad_q = lax.scan(one_block, (empty_kv, empty_kv), members)
    return (grad_q.reshape(length_q, heads_here, head_width), grad_keys, grad_values)


def adapter_forward(normed_input, down_one, up_one, n_head, group_w):
    rows_n, piece_n, model_width = normed_input.shape
    inner_low = lax.dot_general(
        normed_input.reshape(-1, model_width),
        down_one,
        (((1,), (1,)), ((), ())),
        preferred_element_type=jnp.float32,
    )
    inner_low = inner_low.astype(jnp.bfloat16).reshape(rows_n, piece_n, ADAPTER_RANK)
    lifted_rows = ADAPTER_SCALE * jnp.einsum(
        "rts,she->hrte",
        inner_low,
        up_one.reshape(ADAPTER_RANK, n_head, group_w),
        preferred_element_type=jnp.float32,
    )
    return (inner_low, lifted_rows)


def adapter_back(grad_side, inner_low, normed_input, down_one, up_one, n_head, group_w):
    model_width = normed_input.shape[-1]
    up_gradient = ADAPTER_SCALE * jnp.einsum(
        "rts,hrte->she", inner_low, grad_side, preferred_element_type=jnp.float32
    ).reshape(ADAPTER_RANK, model_width)
    grad_inner = (
        ADAPTER_SCALE
        * jnp.einsum(
            "hrte,she->rts",
            grad_side,
            up_one.reshape(ADAPTER_RANK, n_head, group_w),
            preferred_element_type=jnp.float32,
        )
    ).astype(jnp.bfloat16)
    down_gradient = lax.dot_general(
        grad_inner.reshape(-1, ADAPTER_RANK),
        normed_input.reshape(-1, model_width),
        (((0,), (0,)), ((), ())),
        preferred_element_type=jnp.float32,
    )
    grad_normed = jnp.einsum(
        "rts,sd->rtd", grad_inner, down_one, preferred_element_type=jnp.float32
    )
    return (down_gradient, up_gradient, grad_normed)


def attention_forward(
    normed_q,
    normed_kv,
    qkv_w,
    out_w,
    down_low_rank,
    up_low_rank,
    slot_at,
    seg_query,
    seg_key,
    causal,
):
    n_head = lax.axis_size("head")
    rows_n, piece_n, model_width = normed_q.shape
    group_w = model_width // n_head
    heads_here = group_w // HEAD_DIM
    w_query = qkv_w[0].reshape(model_width, n_head, group_w)
    w_pair = qkv_w[1:3].reshape(2, model_width, n_head, group_w)
    inner_q, lifted_q = adapter_forward(
        normed_q, down_low_rank[2 * slot_at], up_low_rank[2 * slot_at], n_head, group_w
    )
    inner_v, lifted_v = adapter_forward(
        normed_kv, down_low_rank[2 * slot_at + 1], up_low_rank[2 * slot_at + 1], n_head, group_w
    )
    queries = (
        jnp.einsum("rtd,dhe->hrte", normed_q, w_query, preferred_element_type=jnp.float32)
        + lifted_q
    )
    pair = jnp.einsum("rtd,kdhe->hrtke", normed_kv, w_pair, preferred_element_type=jnp.float32)
    pair = pair.at[:, :, :, 1].add(lifted_v)
    sent_q = queries.astype(jnp.bfloat16).reshape(n_head * rows_n, piece_n, 1, group_w)
    sent_pair = pair.astype(jnp.bfloat16).reshape(n_head * rows_n, piece_n, 2, group_w)
    got_q, got_pair = (
        lax.all_to_all(sent_q, ("head", "col"), split_axis=0, concat_axis=1, tiled=True),
        lax.all_to_all(sent_pair, ("head", "col"), split_axis=0, concat_axis=1, tiled=True),
    )
    queries_a = got_q.reshape(-1, heads_here, HEAD_DIM)
    keys_a = got_pair[0, :, 0].reshape(-1, heads_here, HEAD_DIM)
    values_a = got_pair[0, :, 1].reshape(-1, heads_here, HEAD_DIM)
    mixed_heads, row_tops, row_sums = attend_forward(
        queries_a, keys_a, values_a, seg_query, seg_key, causal
    )
    back_rows = lax.all_to_all(
        mixed_heads.reshape(1, -1, group_w),
        ("head", "col"),
        split_axis=1,
        concat_axis=0,
        tiled=True,
    )
    back_rows = back_rows.reshape(n_head, rows_n, piece_n, group_w)
    result = jnp.einsum(
        "hrte,hef->rtf",
        back_rows,
        out_w.reshape(n_head, group_w, model_width),
        preferred_element_type=jnp.float32,
    )
    return (result, (inner_q, inner_v, queries_a, keys_a, values_a, row_tops, row_sums))


def attention_backward(
    grad_res,
    normed_q,
    normed_kv,
    kept_fwd,
    qkv_w,
    out_w,
    down_low_rank,
    up_low_rank,
    slot_at,
    seg_query,
    seg_key,
    causal,
):
    inner_q, inner_v, queries_a, keys_a, values_a, row_tops, row_sums = kept_fwd
    n_head = lax.axis_size("head")
    rows_n, piece_n, model_width = normed_q.shape
    group_w = model_width // n_head
    heads_here = group_w // HEAD_DIM
    w_query = qkv_w[0].reshape(model_width, n_head, group_w)
    w_pair = qkv_w[1:3].reshape(2, model_width, n_head, group_w)
    grad_back = jnp.einsum(
        "rtf,hef->hrte",
        grad_res.astype(jnp.bfloat16),
        out_w.reshape(n_head, group_w, model_width),
        preferred_element_type=jnp.float32,
    )
    grad_mixed = lax.all_to_all(
        grad_back.astype(jnp.bfloat16).reshape(n_head * rows_n, piece_n, group_w),
        ("head", "col"),
        split_axis=0,
        concat_axis=1,
        tiled=True,
    )
    grad_q, grad_k, grad_v = attend_backward(
        queries_a,
        keys_a,
        values_a,
        seg_query,
        seg_key,
        causal,
        row_tops,
        row_sums,
        grad_mixed.reshape(-1, heads_here, HEAD_DIM),
    )
    length_q = grad_q.shape[0]
    sent_gq = grad_q.astype(jnp.bfloat16).reshape(1, length_q, 1, group_w)
    sent_gpair = (
        jnp.stack([grad_k, grad_v], axis=1).astype(jnp.bfloat16).reshape(1, length_q, 2, group_w)
    )
    grad_qt, grad_pair = (
        lax.all_to_all(sent_gq, ("head", "col"), split_axis=1, concat_axis=0, tiled=True),
        lax.all_to_all(sent_gpair, ("head", "col"), split_axis=1, concat_axis=0, tiled=True),
    )
    grad_qt = grad_qt.reshape(n_head, rows_n, piece_n, group_w)
    grad_pair = grad_pair.reshape(n_head, rows_n, piece_n, 2, group_w)
    down_query, up_query, side_q = adapter_back(
        grad_qt,
        inner_q,
        normed_q,
        down_low_rank[2 * slot_at],
        up_low_rank[2 * slot_at],
        n_head,
        group_w,
    )
    down_value, up_value, side_v = adapter_back(
        grad_pair[:, :, :, 1],
        inner_v,
        normed_kv,
        down_low_rank[2 * slot_at + 1],
        up_low_rank[2 * slot_at + 1],
        n_head,
        group_w,
    )
    normed_query_gradient = (
        jnp.einsum("hrte,dhe->rtd", grad_qt, w_query, preferred_element_type=jnp.float32) + side_q
    )
    normed_key_value_gradient = (
        jnp.einsum("hrtke,kdhe->rtd", grad_pair, w_pair, preferred_element_type=jnp.float32)
        + side_v
    )
    return (
        normed_query_gradient,
        normed_key_value_gradient,
        (down_query, down_value),
        (up_query, up_value),
    )


def ffn_forward(normed_input, weight_pair):
    model_width = normed_input.shape[-1]
    rows_low = normed_input.reshape(-1, model_width)
    rows_low = col_rows(rows_low)
    pre_act = lax.dot_general(
        rows_low, weight_pair[0], (((1,), (1,)), ((), ())), preferred_element_type=jnp.float32
    )
    hidden = jnp.maximum(pre_act, 0.0).astype(jnp.bfloat16)
    result = jnp.dot(hidden, weight_pair[1], preferred_element_type=jnp.float32)
    result = col_sums(result)
    return (result.reshape(normed_input.shape), (pre_act > 0.0, weight_pair))


def ffn_backward(grad_res, kept_fwd):
    active, matrices = kept_fwd
    model_width = grad_res.shape[-1]
    grad_low = grad_res.reshape(-1, model_width).astype(jnp.bfloat16)
    grad_low = col_rows(grad_low)
    grad_hidden = lax.dot_general(
        grad_low, matrices[1], (((1,), (1,)), ((), ())), preferred_element_type=jnp.float32
    )
    grad_pre = jnp.where(active, grad_hidden, 0.0).astype(jnp.bfloat16)
    grad_in = jnp.dot(grad_pre, matrices[0], preferred_element_type=jnp.float32)
    grad_in = col_sums(grad_in)
    return grad_in.reshape(grad_res.shape)


def vocab_stats(head_rows, clipped, inside, embedding, n_col):
    model_width = head_rows.shape[1]

    def one_block(members):
        rows_blk, clip_blk, inside_blk = members
        logits = lax.dot_general(
            rows_blk, embedding, (((1,), (1,)), ((), ())), preferred_element_type=jnp.float32
        )
        row_top = jnp.max(logits, axis=1)
        row_total = jnp.sum(jnp.exp(logits - row_top[:, None]), axis=1)
        picked = jnp.take_along_axis(logits, clip_blk[:, None], axis=1)[:, 0]
        return (row_top, row_total, jnp.where(inside_blk, picked, 0.0))

    block_outs = lax.map(
        one_block,
        (
            head_rows.reshape(n_col, -1, model_width),
            clipped.reshape(n_col, -1),
            inside.reshape(n_col, -1),
        ),
    )
    return tuple((member.reshape(-1) for member in block_outs))


def vocab_back(head_rows, clipped, inside, embedding, n_col, log_total, coef_rows):
    model_width = head_rows.shape[1]
    vocab_part = embedding.shape[0]

    def one_block(members):
        rows_blk, clip_blk, inside_blk, total_blk, coef_blk = members
        logits = lax.dot_general(
            rows_blk, embedding, (((1,), (1,)), ((), ())), preferred_element_type=jnp.float32
        )
        probs_f = jnp.exp(logits - total_blk[:, None])
        hits = (jnp.arange(vocab_part, dtype=jnp.int32)[None, :] == clip_blk[:, None]) & inside_blk[
            :, None
        ]
        grad_logits = (coef_blk[:, None] * (probs_f - hits.astype(jnp.float32))).astype(
            jnp.bfloat16
        )
        return jnp.dot(grad_logits, embedding, preferred_element_type=jnp.float32)

    members = (
        head_rows.reshape(n_col, -1, model_width),
        clipped.reshape(n_col, -1),
        inside.reshape(n_col, -1),
        log_total.reshape(n_col, -1),
        coef_rows.reshape(n_col, -1),
    )
    return lax.map(one_block, members).reshape(-1, model_width)


def merge_stats(left_side, right_side):
    top_both = jnp.maximum(left_side[0], right_side[0])
    summed = left_side[1] * jnp.exp(left_side[0] - top_both) + right_side[1] * jnp.exp(
        right_side[0] - top_both
    )
    return (top_both, summed, left_side[2] + right_side[2])


def adam_update(weights, gradient, first_moment, second_moment, step_rate, step_count_float):
    first_new = BETA_ONE * first_moment + (1.0 - BETA_ONE) * gradient
    second_new = BETA_TWO * second_moment + (1.0 - BETA_TWO) * gradient * gradient
    first_hat = first_new / (1.0 - BETA_ONE**step_count_float)
    second_hat = second_new / (1.0 - BETA_TWO**step_count_float)
    weights_new = weights - step_rate * (
        first_hat / (jnp.sqrt(second_hat) + ADAM_EPS) + DECAY * weights
    )
    return (weights_new, first_new, second_new)


def per_device(
    encoder_token_ids,
    decoder_token_ids,
    target_token_ids,
    target_count_mask,
    encoder_document_length,
    decoder_document_length,
    embedding,
    attention_projection_weight,
    attention_output_weight,
    feedforward_weight,
    norm_gain_rows,
    earlier_down_weight,
    adapter_down_weight,
    adapter_up_weight,
    down_first_moment,
    down_second_moment,
    up_first_moment,
    up_second_moment,
    optimizer_step_count,
):
    n_col = lax.axis_size("col")
    col_at = lax.axis_index("col")
    rows_n, piece_n = encoder_token_ids.shape
    vocab_part, model_width = embedding.shape
    gathered = (
        lax.all_gather(encoder_token_ids, "col", axis=0, tiled=True),
        lax.all_gather(decoder_token_ids, "col", axis=0, tiled=True),
        lax.all_gather(target_token_ids, "col", axis=0, tiled=True),
        lax.all_gather(target_count_mask, "col", axis=0, tiled=True),
    )
    enc_all, dec_all, target_all, mask_all = [member.reshape(-1) for member in gathered]

    def lookup(ids_flat):
        local_ids = ids_flat - col_at * vocab_part
        inside_ids = (local_ids >= 0) & (local_ids < vocab_part)
        picked = jnp.take(embedding, jnp.clip(local_ids, 0, vocab_part - 1), axis=0).astype(
            jnp.float32
        )
        return jnp.where(inside_ids[:, None], picked, 0.0)

    embedded = col_sums(jnp.stack([lookup(enc_all), lookup(dec_all)], axis=1))
    enc_state = embedded[:, 0].reshape(rows_n, piece_n, model_width)
    dec_state = embedded[:, 1].reshape(rows_n, piece_n, model_width)
    down_low_rank = adapter_down_weight.astype(jnp.bfloat16)
    up_low_rank = adapter_up_weight.astype(jnp.bfloat16)
    enc_seg = segment_of(
        lax.dynamic_index_in_dim(encoder_document_length, col_at, 0, keepdims=False), LEN
    )
    dec_seg = segment_of(
        lax.dynamic_index_in_dim(decoder_document_length, col_at, 0, keepdims=False), LEN
    )
    enc_normed = rms_norm(enc_state, norm_gain_rows[0]).astype(jnp.bfloat16)
    branch_out, kept_enc = attention_forward(
        enc_normed,
        enc_normed,
        attention_projection_weight[0],
        attention_output_weight[0],
        down_low_rank,
        up_low_rank,
        0,
        enc_seg,
        enc_seg,
        False,
    )
    enc_mid = enc_state + branch_out
    branch_out, ffn_enc = ffn_forward(
        rms_norm(enc_mid, norm_gain_rows[1]).astype(jnp.bfloat16), feedforward_weight[0]
    )
    enc_last = enc_mid + branch_out
    encoded = rms_norm(enc_last, norm_gain_rows[2]).astype(jnp.bfloat16)
    dec_normed = rms_norm(dec_state, norm_gain_rows[3]).astype(jnp.bfloat16)
    branch_out, kept_self = attention_forward(
        dec_normed,
        dec_normed,
        attention_projection_weight[1],
        attention_output_weight[1],
        down_low_rank,
        up_low_rank,
        1,
        dec_seg,
        dec_seg,
        True,
    )
    dec_one = dec_state + branch_out
    cross_normed = rms_norm(dec_one, norm_gain_rows[4]).astype(jnp.bfloat16)
    branch_out, kept_cross = attention_forward(
        cross_normed,
        encoded,
        attention_projection_weight[2],
        attention_output_weight[2],
        down_low_rank,
        up_low_rank,
        2,
        dec_seg,
        enc_seg,
        False,
    )
    dec_two = dec_one + branch_out
    branch_out, ffn_dec = ffn_forward(
        rms_norm(dec_two, norm_gain_rows[5]).astype(jnp.bfloat16), feedforward_weight[1]
    )
    dec_three = dec_two + branch_out
    head_scale = MODEL_DIMENSION ** (-0.5)
    final_rows = (rms_norm(dec_three, norm_gain_rows[6]) * head_scale).astype(jnp.bfloat16)
    head_rows = col_rows(final_rows.reshape(-1, model_width))
    local_t = target_all - col_at * vocab_part
    inside = (local_t >= 0) & (local_t < vocab_part)
    clipped = jnp.clip(local_t, 0, vocab_part - 1)
    top_part, sum_part, target_part = vocab_stats(head_rows, clipped, inside, embedding, n_col)
    row_top, row_total, row_target = joined((top_part, sum_part, target_part), "col", merge_stats)
    log_total = row_top + jnp.log(row_total)
    mask_float = mask_all.astype(jnp.float32)
    ce_local = jnp.sum(mask_float * (log_total - row_target))
    count_local = jnp.sum(mask_float)
    ce_total, target_count = lax.psum((ce_local, count_local), ("dp", "head"))
    grad_rows = vocab_back(
        head_rows, clipped, inside, embedding, n_col, log_total, mask_float / target_count
    )
    grad_final = col_sums(grad_rows).reshape(rows_n, piece_n, model_width)
    grad_dec = norm_back(dec_three, norm_gain_rows[6], grad_final, head_scale)
    grad_dec = grad_dec + norm_back(
        dec_two, norm_gain_rows[5], ffn_backward(grad_dec, ffn_dec), 1.0
    )
    normed_query_gradient, grad_encoded, downs_cross, ups_cross = attention_backward(
        grad_dec,
        cross_normed,
        encoded,
        kept_cross,
        attention_projection_weight[2],
        attention_output_weight[2],
        down_low_rank,
        up_low_rank,
        2,
        dec_seg,
        enc_seg,
        False,
    )
    grad_dec = grad_dec + norm_back(dec_one, norm_gain_rows[4], normed_query_gradient, 1.0)
    unused_q, unused_kv, downs_self, ups_self = attention_backward(
        grad_dec,
        dec_normed,
        dec_normed,
        kept_self,
        attention_projection_weight[1],
        attention_output_weight[1],
        down_low_rank,
        up_low_rank,
        1,
        dec_seg,
        dec_seg,
        True,
    )
    grad_enc = norm_back(enc_last, norm_gain_rows[2], grad_encoded, 1.0)
    grad_enc = grad_enc + norm_back(
        enc_mid, norm_gain_rows[1], ffn_backward(grad_enc, ffn_enc), 1.0
    )
    unused_q, unused_kv, downs_enc, ups_enc = attention_backward(
        grad_enc,
        enc_normed,
        enc_normed,
        kept_enc,
        attention_projection_weight[0],
        attention_output_weight[0],
        down_low_rank,
        up_low_rank,
        0,
        enc_seg,
        enc_seg,
        False,
    )
    down_gradient = jnp.stack(
        [downs_enc[0], downs_enc[1], downs_self[0], downs_self[1], downs_cross[0], downs_cross[1]]
    )
    up_gradient = jnp.stack(
        [ups_enc[0], ups_enc[1], ups_self[0], ups_self[1], ups_cross[0], ups_cross[1]]
    )
    down_penalty_sum, up_penalty_sum = lax.psum((down_gradient, up_gradient), ("dp", "head", "col"))
    earlier_down_float = earlier_down_weight.astype(jnp.float32)
    intersection = jnp.einsum(
        "hygm,hvm->hygv", earlier_down_float, adapter_down_weight, precision=lax.Precision.HIGHEST
    )
    penalty = ORTH_WEIGHT * jnp.sum(intersection * intersection) + BASE_NORM_WEIGHT * jnp.sum(
        adapter_up_weight * adapter_up_weight
    )
    down_penalty_sum = down_penalty_sum + 2.0 * ORTH_WEIGHT * jnp.einsum(
        "aoij,aoid->ajd", intersection, earlier_down_float, precision=lax.Precision.HIGHEST
    )
    up_penalty_sum = up_penalty_sum + 2.0 * BASE_NORM_WEIGHT * adapter_up_weight
    loss_scalar = ce_total / target_count + penalty
    step_count_float = optimizer_step_count[0].astype(jnp.float32)
    updated_down_weight, down_first_updated, down_second_updated = adam_update(
        adapter_down_weight,
        down_penalty_sum,
        down_first_moment,
        down_second_moment,
        DOWN_STEP_RATE,
        step_count_float,
    )
    updated_up_weight, up_first_updated, up_second_updated = adam_update(
        adapter_up_weight,
        up_penalty_sum,
        up_first_moment,
        up_second_moment,
        UP_STEP_RATE,
        step_count_float,
    )
    return (
        loss_scalar,
        updated_down_weight,
        down_first_updated,
        down_second_updated,
        updated_up_weight,
        up_first_updated,
        up_second_updated,
    )


def solution(mesh):
    in_specs = (
        P("dp", ("head", "col")),
        P("dp", ("head", "col")),
        P("dp", ("head", "col")),
        P("dp", ("head", "col")),
        P("dp", None),
        P("dp", None),
        P("col", None),
        P(),
        P(),
        P(None, None, "col", None),
        P(),
        P(),
        P(),
        P(),
        P(),
        P(),
        P(),
        P(),
        P(),
    )
    out_specs = (P(), P(), P(), P(), P(), P(), P())
    return jax.shard_map(
        per_device, mesh=mesh, in_specs=in_specs, out_specs=out_specs, check_vma=False
    )
```

profile of v0, /device:TPU:0, one launch (start us, length us, event | category | flops | bytes accessed | tf_op | source)
XLA Modules:
  0.0 1621.3 jit_solution(584099909440512149)
XLA Ops:
  7.2 13.9 all-gather.1
  21.1 12.1 all-gather.2
  33.5 11.7 gather_fusion.2
  45.2 10.6 gather_fusion.1
  63.4 5.8 fusion.340
  81.3 90.1 %reduce-scatter.7.cloned.1.call-done = f32[256,2,768]{2,0,1:T(8,128)} async-done(((f32[1024,2,768]{2,0,1:T(8,128)}), f32[256,2,768]{2,0,1:T(8,128)}) %reduce-scatter.7.cloned.1.call-update) | async-done | bytes 1572880 | tf_op jit(solution)/shard_map/reduce_scatter | solution.py:58
  180.1 5.3 all-to-all-start.4
  191.3 9.7 all-to-all-done.4
  221.9 10.8 all-to-all-done.5
  236.3 11.6 while.134
  251.2 4.9 reduce.27
  264.5 9.3 all-to-all-done.6
  288.0 5.6 all-to-all-done
  298.0 8.8 reduce-scatter.9.cloned.1.call-start
  311.9 33.2 %all-to-all-done.1 = bf16[16,64,2,192]{3,1,2,0:T(8,128)(2,1)} async-done(((bf16[16,64,2,192]{3,1,2,0:T(8,128)(2,1)}), bf16[16,64,2,192]{3,1,2,0:T(8,128)(2,1)}, u32[]{:S(2)}, u32[]{:S(2)}) %all-to-all-start.1) | async-done | bytes 786464 | tf_op jit(solution)/shard_map/all_to_all | solution.py:229
  357.9 14.6 while.133
  377.0 4.9 reduce.26
  393.2 17.8 %all-to-all-done.2 = bf16[16,2,6144]{2,1,0:T(2,128)(2,1)S(1)} async-done(((bf16[16,2,6144]{2,1,0:T(2,128)(2,1)}), bf16[16,2,6144]{2,1,0:T(2,128)(2,1)S(1)}, u32[]{:S(2)}, u32[]{:S(2)}) %all-to-all-start.2) | async-done | bytes 393248 | tf_op jit(solution)/shard_map/all_to_all | solution.py:237
  444.9 24.2 %all-to-all-done.7 = bf16[16,64,2,192]{3,1,2,0:T(8,128)(2,1)} async-done(((bf16[16,64,2,192]{3,1,2,0:T(8,128)(2,1)}), bf16[16,64,2,192]{3,1,2,0:T(8,128)(2,1)}, u32[]{:S(2)}, u32[]{:S(2)}) %all-to-all-start.7) | async-done | bytes 786464 | tf_op jit(solution)/shard_map/all_to_all | solution.py:229
  472.7 11.6 while.135
  488.8 4.9 reduce.28
  495.0 16.3 %all_to_all.81 = bf16[16,2,6144]{2,1,0:T(2,128)(2,1)S(1)} all-to-all(bf16[16,2,6144]{2,1,0:T(2,128)(2,1)} %reshape.1380), channel_id=1, replica_groups=mesh['dp'=2,'head'=4,'col'=4] {'head','col'}, dimensions={0} | all-to-all | bytes 786432 | tf_op jit(solution)/shard_map/all_to_all | solution.py:237
  517.9 35.5 %all-gather.15.cloned.1.call-done = bf16[1024,768]{1,0:T(8,128)(2,1)} async-done(((bf16[256,768]{1,0:T(8,128)(2,1)}), bf16[1024,768]{1,0:T(8,128)(2,1)}) %all-gather.15.cloned.1.call-update) | async-done | bytes 1572880 | tf_op jit(solution)/shard_map/all_gather | solution.py:54
  562.6 59.4 %reduce-scatter.11.cloned.1.call-done = f32[256,768]{1,0:T(8,128)} async-done(((f32[1024,768]{1,0:T(8,128)}), f32[256,768]{1,0:T(8,128)}) %reduce-scatter.11.cloned.1.call-update) | async-done | bytes 786448 | tf_op jit(solution)/shard_map/reduce_scatter | solution.py:58
  624.4 12.0 all-gather.3
  636.6 12.4 all-gather
  649.7 11.8 all-gather.17.cloned.1.call-done
  661.5 94.4 %while.136 = (s32[]{:T(128)}, f32[4,256]{1,0:T(4,128)S(1)}, f32[4,256]{1,0:T(4,128)S(1)}, f32[4,256]{1,0:T(4,128)S(1)}, bf16[4,256,768]{2,1,0:T(8,128)(2,1)}, /*...) while((s32[]{:T(128)}, f32[4,256]{1,0:T(4,128)S(1)}, ...), condition=%wide.region_29.31_spmd, body=%wide.region_26.30_spmd.sunk | while | flops 3164483584 | bytes 29207416 | solution.py:383
  661.5 11.4 fusion.495
  673.0 7.7 gather_fusion
  685.3 11.4 fusion.495
  696.7 7.7 gather_fusion
  709.1 11.4 fusion.495
  720.5 7.4 gather_fusion
  732.6 11.4 fusion.495
  744.0 7.4 gather_fusion
  756.0 13.2 all-gather.4
  769.2 13.2 all-gather.5
  782.5 13.2 all-gather.6
  796.6 12.6 all-reduce.1
  809.9 85.9 %while.138 = (s32[]{:T(128)}, f32[4,256,768]{2,1,0:T(8,128)}, f32[4,256]{1,0:T(4,128)S(1)}, bf16[4,256,768]{2,1,0:T(8,128)(2,1)}, bf16[8032,768]{1,0:T(8,128)(2,...) while((s32[]{:T(128)}, f32[4,256,768]{2,1,0:T(8,128)}, ...), condition=%wide.region_39.41_spmd, body=%wide.region_38.40_spmd.sunk | while | flops 6331015168 | bytes 25865064 | solution.py:419
  810.0 21.4 %fusion.500 = f32[4,256,768]{2,1,0:T(8,128)} fusion(f32[4,256,768]{2,1,0:T(8,128)} %get-tuple-element.2170, s32[]{:T(128)} %get-tuple-element.2169, bf16[8032,768]{1,0:T(8,128)(2,1)} %get-tuple-element.2182, s32[256]{0:T(256)S(1)} %bitcast.1124, f32[256]{0:T(256)S(1)} %bitcast.1125, f32[256]{0:T(256)S(1)} %bitcast.1126, ...), kind=kOutput, calls=%fused_computation.187.clone.1 | convolution fusion | flops 6331015168 | bytes 25858304 | tf_op jit(solution)/shard_map/while/body/eval_jaxpr/dot_general | solution.py:410
  831.4 21.4 %fusion.500 = f32[4,256,768]{2,1,0:T(8,128)} fusion(f32[4,256,768]{2,1,0:T(8,128)} %get-tuple-element.2170, s32[]{:T(128)} %get-tuple-element.2169, bf16[8032,768]{1,0:T(8,128)(2,1)} %get-tuple-element.2182, s32[256]{0:T(256)S(1)} %bitcast.1124, f32[256]{0:T(256)S(1)} %bitcast.1125, f32[256]{0:T(256)S(1)} %bitcast.1126, ...), kind=kOutput, calls=%fused_computation.187.clone.1 | convolution fusion | flops 6331015168 | bytes 25858304 | tf_op jit(solution)/shard_map/while/body/eval_jaxpr/dot_general | solution.py:410
  852.9 21.4 %fusion.500 = f32[4,256,768]{2,1,0:T(8,128)} fusion(f32[4,256,768]{2,1,0:T(8,128)} %get-tuple-element.2170, s32[]{:T(128)} %get-tuple-element.2169, bf16[8032,768]{1,0:T(8,128)(2,1)} %get-tuple-element.2182, s32[256]{0:T(256)S(1)} %bitcast.1124, f32[256]{0:T(256)S(1)} %bitcast.1125, f32[256]{0:T(256)S(1)} %bitcast.1126, ...), kind=kOutput, calls=%fused_computation.187.clone.1 | convolution fusion | flops 6331015168 | bytes 25858304 | tf_op jit(solution)/shard_map/while/body/eval_jaxpr/dot_general | solution.py:410
  874.4 21.4 %fusion.500 = f32[4,256,768]{2,1,0:T(8,128)} fusion(f32[4,256,768]{2,1,0:T(8,128)} %get-tuple-element.2170, s32[]{:T(128)} %get-tuple-element.2169, bf16[8032,768]{1,0:T(8,128)(2,1)} %get-tuple-element.2182, s32[256]{0:T(256)S(1)} %bitcast.1124, f32[256]{0:T(256)S(1)} %bitcast.1125, f32[256]{0:T(256)S(1)} %bitcast.1126, ...), kind=kOutput, calls=%fused_computation.187.clone.1 | convolution fusion | flops 6331015168 | bytes 25858304 | tf_op jit(solution)/shard_map/while/body/eval_jaxpr/dot_general | solution.py:410
  895.9 59.4 %reduce-scatter.13.cloned.1.call-done = f32[256,768]{1,0:T(8,128)} async-done(((f32[1024,768]{1,0:T(8,128)}), f32[256,768]{1,0:T(8,128)}) %reduce-scatter.13.cloned.1.call-update) | async-done | bytes 786448 | tf_op jit(solution)/shard_map/reduce_scatter | solution.py:58
  958.8 37.0 %all-gather.19.cloned.1.call-done = bf16[1024,768]{1,0:T(8,128)(2,1)} async-done(((bf16[256,768]{1,0:T(8,128)(2,1)}), bf16[1024,768]{1,0:T(8,128)(2,1)}) %all-gather.19.cloned.1.call-update) | async-done | bytes 1572880 | tf_op jit(solution)/shard_map/all_gather | solution.py:54
  995.8 7.4 fusion.175
  1003.3 59.4 %reduce-scatter.15.cloned.1.call-done = f32[256,768]{1,0:T(8,128)} async-done(((f32[1024,768]{1,0:T(8,128)}), f32[256,768]{1,0:T(8,128)}) %reduce-scatter.15.cloned.1.call-update) | async-done | bytes 786448 | tf_op jit(solution)/shard_map/reduce_scatter | solution.py:58
  1072.7 15.3 all-to-all-done.9
  1094.2 31.6 %while.139 = (s32[]{:T(128)}, f32[1024,3,64]{0,2,1:T(8,128)S(1)}, f32[1024,3,64]{0,2,1:T(8,128)S(1)}, bf16[2,512,3,64]{1,3,2,0:T(8,128)(2,1)}, bf16[2,512,3,64]{...) while((s32[]{:T(128)}, f32[1024,3,64]{0,2,1:T(8,128)S(1)}, ...), condition=%wide.region_46.48_spmd.clone, body=%wide.region_44.47_spmd.clone.sunk | while | flops 1023965696 | bytes 107278104 | solution.py:147
  1127.0 30.2 %all_to_all.82 = bf16[1,1024,2,192]{3,2,0,1:T(2,128)(2,1)S(1)} all-to-all(bf16[1,1024,2,192]{3,2,0,1:T(2,128)(2,1)S(1)} %copy.502), channel_id=1, replica_groups=mesh['dp'=2,'head'=4,'col'=4] {'head','col'}, dimensions={1} | all-to-all | bytes 1572864 | tf_op jit(solution)/shard_map/all_to_all | solution.py:306
  1162.1 35.4 %all-gather.21.cloned.1.call-done = bf16[1024,768]{1,0:T(8,128)(2,1)} async-done(((bf16[256,768]{1,0:T(8,128)(2,1)}), bf16[1024,768]{1,0:T(8,128)(2,1)}) %all-gather.21.cloned.1.call-update) | async-done | bytes 1572880 | tf_op jit(solution)/shard_map/all_gather | solution.py:54
  1197.6 7.4 fusion.181
  1208.7 5.3 reduce.30
  1214.5 27.2 %all_to_all.83 = bf16[16,2,6144]{2,1,0:T(2,128)(2,1)} all-to-all(bf16[16,2,6144]{2,1,0:T(2,128)(2,1)S(1)} %reshape.1384), channel_id=1, replica_groups=mesh['dp'=2,'head'=4,'col'=4] {'head','col'}, dimensions={0} | all-to-all | bytes 786432 | tf_op jit(solution)/shard_map/all_to_all | solution.py:305
  1254.2 28.0 %all-to-all-done.15 = bf16[16,64,192]{2,1,0:T(8,128)(2,1)S(1)} async-done(((bf16[16,64,192]{2,1,0:T(8,128)(2,1)}), bf16[16,64,192]{2,1,0:T(8,128)(2,1)S(1)}, u32[]{:S(2)}, u32[]{:S(2)}) %all-to-all-start.15) | async-done | bytes 393248 | tf_op jit(solution)/shard_map/all_to_all | solution.py:281
  1296.4 34.7 %while.141 = (s32[]{:T(128)}, f32[1024,3,64]{0,2,1:T(8,128)S(1)}, f32[1024,3,64]{0,2,1:T(8,128)S(1)}, bf16[2,512,3,64]{1,3,2,0:T(8,128)(2,1)}, bf16[2,512,3,64]{...) while((s32[]{:T(128)}, f32[1024,3,64]{0,2,1:T(8,128)S(1)}, ...), condition=%wide.region_56.58_spmd.clone, body=%wide.region_54.57_spmd.clone.sunk | while | flops 1025014784 | bytes 107282224 | solution.py:147
  1335.1 4.9 reduce.31
  1341.3 6.1 all-to-all-start.16
  1365.6 31.8 %while.140 = (s32[]{:T(128)}, f32[1024,3,64]{0,2,1:T(8,128)S(1)}, f32[1024,3,64]{0,2,1:T(8,128)S(1)}, bf16[2,512,3,64]{1,3,2,0:T(8,128)(2,1)}, bf16[2,512,3,64]{...) while((s32[]{:T(128)}, f32[1024,3,64]{0,2,1:T(8,128)S(1)}, ...), condition=%wide.region_52.54_spmd.clone, body=%wide.region_50.53_spmd.clone.sunk | while | flops 1023965696 | bytes 107278104 | solution.py:147
  1407.3 6.1 all-to-all-start.12
  1415.6 10.6 all-to-all-done.12
  1485.0 122.7 %all-reduce.4.cloned.1.call-done = (f32[6,8,768]{2,1,0:T(8,128)}, f32[6,8,768]{2,1,0:T(8,128)}) async-done(((f32[6,8,768]{2,1,0:T(8,128)}, f32[6,8,768]{2,1,0:T(8,128)}), (f32[6,8,768]{2,1,0:T(8,128)}, f32[6,8,768]{2,1,0:T(8,128)})) %all-reduce.4.cloned.1.call-update) | async-done | bytes 294928 | tf_op jit(solution)/shard_map/psum | solution.py:618
  (789 shorter events, 492.1 us)
Async XLA Ops:
  7.2 1474.3 %copy-start = (bf16[6,14,8,768]{3,2,1,0:T(8,128)(2,1)S(1)}, bf16[6,14,8,768]{3,2,1,0:T(8,128)(2,1)}, u32[]{:S(2)}) copy-start(bf16[6,14,8,768]{3,2,1,0:T(8,128)(2,1)} %param.56) | copy-start | bytes 3096580
  7.2 164.2 %reduce-scatter.7.cloned.1.call-start = ((), (), s32[]{:S(2)}) async-start(), calls=%async_computation.24 | async-start | bytes 7864320 | tf_op jit(solution)/shard_map/reduce_scatter | solution.py:58
  74.2 115.5 %copy-start.78 = (bf16[8,4,192]{2,1,0:T(4,128)(2,1)}, bf16[8,4,192]{2,1,0:T(4,128)(2,1)S(1)}, u32[]{:S(2)}) copy-start(bf16[8,4,192]{2,1,0:T(4,128)(2,1)S(1)} %reshape_squeeze.82) | copy-start | bytes 36868
  74.3 102.5 %copy-start.80 = (bf16[8,4,192]{2,1,0:T(4,128)(2,1)}, bf16[8,4,192]{2,1,0:T(4,128)(2,1)S(1)}, u32[]{:S(2)}) copy-start(bf16[8,4,192]{2,1,0:T(4,128)(2,1)S(1)} %reshape_squeeze.81) | copy-start | bytes 36868
  80.6 95.9 %copy-start.67 = (bf16[6,8,768]{2,1,0:T(8,128)(2,1)S(1)}, bf16[6,8,768]{2,1,0:T(8,128)(2,1)}, u32[]{:S(2)}) copy-start(bf16[6,8,768]{2,1,0:T(8,128)(2,1)} %convert_element_type.311) | copy-start | bytes 221188
  81.3 94.5 %copy-start.102 = (f32[768]{0:T(1024)}, f32[768]{0:T(1024)S(1)}, u32[]{:S(2)}) copy-start(f32[768]{0:T(1024)S(1)} %get-tuple-element.1132) | copy-start | bytes 9220
  81.3 96.0 %copy-start.101 = (f32[768]{0:T(1024)}, f32[768]{0:T(1024)S(1)}, u32[]{:S(2)}) copy-start(f32[768]{0:T(1024)S(1)} %get-tuple-element.1134) | copy-start | bytes 9220
  81.3 201.2 %copy-start.106 = (f32[768]{0:T(1024)}, f32[768]{0:T(1024)S(1)}, u32[]{:S(2)}) copy-start(f32[768]{0:T(1024)S(1)} %get-tuple-element.1131) | copy-start | bytes 9220
  180.1 20.9 %all-to-all-start.4 = ((bf16[16,64,1,192]{3,1,2,0:T(8,128)(2,1)}), bf16[16,64,1,192]{3,1,2,0:T(8,128)(2,1)}, u32[]{:S(2)}, u32[]{:S(2)}) async-start(bf16[16,64,1,192]{3,1,2,0:T(8,128)(2,1)} %bitcast.1076), calls=%async_computation.5 | async-start | bytes 1048576 | tf_op jit(solution)/shard_map/all_to_all | solution.py:228
  201.0 31.6 %all-to-all-start.5 = ((bf16[16,64,2,192]{3,1,2,0:T(8,128)(2,1)}), bf16[16,64,2,192]{3,1,2,0:T(8,128)(2,1)}, u32[]{:S(2)}, u32[]{:S(2)}) async-start(bf16[16,64,2,192]{3,1,2,0:T(8,128)(2,1)} %bitcast.1042), calls=%async_computation.6 | async-start | bytes 2097152 | tf_op jit(solution)/shard_map/all_to_all | solution.py:229
  209.8 76.7 %copy-start.82 = (bf16[8,4,192]{2,1,0:T(4,128)(2,1)}, bf16[8,4,192]{2,1,0:T(4,128)(2,1)S(1)}, u32[]{:S(2)}) copy-start(bf16[8,4,192]{2,1,0:T(4,128)(2,1)S(1)} %reshape_squeeze.73) | copy-start | bytes 36868
  217.1 69.4 %copy-start.97 = (bf16[4,64,8]{1,0,2:T(4,128)(2,1)}, bf16[4,64,8]{1,0,2:T(4,128)(2,1)S(1)}, u32[]{:S(2)}) copy-start(bf16[4,64,8]{1,0,2:T(4,128)(2,1)S(1)} %reshape.1161) | copy-start | bytes 12292
  257.5 16.3 %all-to-all-start.6 = ((bf16[16,2,6144]{2,1,0:T(2,128)(2,1)}), bf16[16,2,6144]{2,1,0:T(2,128)(2,1)S(1)}, u32[]{:S(2)}, u32[]{:S(2)}) async-start(bf16[16,2,6144]{2,1,0:T(2,128)(2,1)} %reshape.1378), calls=%async_computation.7 | async-start | bytes 786432 | tf_op jit(solution)/shard_map/all_to_all | solution.py:237
  273.8 19.8 %all-to-all-start = ((bf16[16,64,1,192]{3,1,2,0:T(8,128)(2,1)}), bf16[16,64,1,192]{3,1,2,0:T(8,128)(2,1)}, u32[]{:S(2)}, u32[]{:S(2)}) async-start(bf16[16,64,1,192]{3,1,2,0:T(8,128)(2,1)} %bitcast.53), calls=%async_computation.1 | async-start | bytes 1048576 | tf_op jit(solution)/shard_map/all_to_all | solution.py:228
  278.1 70.5 %all-gather.13.cloned.1.call-start = ((), (), s32[]{:S(2)}) async-start(), calls=%async_computation.25 | async-start | bytes 1966080 | tf_op jit(solution)/shard_map/all_gather | solution.py:54
  282.5 140.1 %copy-start.15 = (f32[4,64,768]{2,1,0:T(8,128)}, f32[4,64,768]{2,1,0:T(8,128)S(1)}, u32[]{:S(2)}) copy-start(f32[4,64,768]{2,1,0:T(8,128)S(1)} %get-tuple-element.1391) | copy-start | bytes 2359300
  286.8 20.0 %copy-start.139 = (s32[4,1]{0,1:T(1,128)S(1)}, s32[4,1]{0,1:T(1,128)}, u32[]{:S(2)}) copy-start(s32[4,1]{0,1:T(1,128)} %get-tuple-element.1404) | copy-start | bytes 52
  293.7 51.4 %all-to-all-start.1 = ((bf16[16,64,2,192]{3,1,2,0:T(8,128)(2,1)}), bf16[16,64,2,192]{3,1,2,0:T(8,128)(2,1)}, u32[]{:S(2)}, u32[]{:S(2)}) async-start(bf16[16,64,2,192]{3,1,2,0:T(8,128)(2,1)} %bitcast.66), calls=%async_computation.2 | async-start | bytes 2097152 | tf_op jit(solution)/shard_map/all_to_all | solution.py:229
  298.0 124.6 %reduce-scatter.9.cloned.1.call-start = ((), (), s32[]{:S(2)}) async-start(), calls=%async_computation.26 | async-start | bytes 3932160 | tf_op jit(solution)/shard_map/reduce_scatter | solution.py:58
  383.3 27.7 %all-to-all-start.2 = ((bf16[16,2,6144]{2,1,0:T(2,128)(2,1)}), bf16[16,2,6144]{2,1,0:T(2,128)(2,1)S(1)}, u32[]{:S(2)}, u32[]{:S(2)}) async-start(bf16[16,2,6144]{2,1,0:T(2,128)(2,1)} %reshape.1376), calls=%async_computation.3 | async-start | bytes 786432 | tf_op jit(solution)/shard_map/all_to_all | solution.py:237
  391.6 38.2 %copy-start.104 = (bf16[8,4,192]{2,1,0:T(4,128)(2,1)}, bf16[8,4,192]{2,1,0:T(4,128)(2,1)S(1)}, u32[]{:S(2)}) copy-start(bf16[8,4,192]{2,1,0:T(4,128)(2,1)S(1)} %reshape_squeeze.86) | copy-start | bytes 36868
  391.7 23.8 %copy-start.85 = (bf16[8,4,192]{2,1,0:T(4,128)(2,1)}, bf16[8,4,192]{2,1,0:T(4,128)(2,1)S(1)}, u32[]{:S(2)}) copy-start(bf16[8,4,192]{2,1,0:T(4,128)(2,1)S(1)} %reshape_squeeze.78) | copy-start | bytes 36868
  393.2 20.8 %copy-start.113 = (f32[768]{0:T(1024)S(1)}, f32[768]{0:T(1024)}, u32[]{:S(2)}) copy-start(f32[768]{0:T(1024)} %get-tuple-element.1133) | copy-start | bytes 9220
  413.9 100.7 %copy-start.13 = (f32[4,64,768]{2,1,0:T(8,128)}, f32[4,64,768]{2,1,0:T(8,128)S(1)}, u32[]{:S(2)}) copy-start(f32[4,64,768]{2,1,0:T(8,128)S(1)} %get-tuple-element.1389) | copy-start | bytes 2359300
  418.7 19.1 %all-to-all-start.3 = ((bf16[16,64,1,192]{3,1,2,0:T(8,128)(2,1)}), bf16[16,64,1,192]{3,1,2,0:T(8,128)(2,1)S(1)}, u32[]{:S(2)}, u32[]{:S(2)}) async-start(bf16[16,64,1,192]{3,1,2,0:T(8,128)(2,1)} %bitcast.1075), calls=%async_computation.4 | async-start | bytes 1048576 | tf_op jit(solution)/shard_map/all_to_all | solution.py:228
  437.8 31.2 %all-to-all-start.7 = ((bf16[16,64,2,192]{3,1,2,0:T(8,128)(2,1)}), bf16[16,64,2,192]{3,1,2,0:T(8,128)(2,1)}, u32[]{:S(2)}, u32[]{:S(2)}) async-start(bf16[16,64,2,192]{3,1,2,0:T(8,128)(2,1)} %bitcast.137), calls=%async_computation.9 | async-start | bytes 2097152 | tf_op jit(solution)/shard_map/all_to_all | solution.py:229
  442.1 111.2 %all-gather.15.cloned.1.call-start = ((), (), s32[]{:S(2)}) async-start(), calls=%async_computation.27 | async-start | bytes 1966080 | tf_op jit(solution)/shard_map/all_gather | solution.py:54
  484.3 27.0 %copy-start.22 = (bf16[1024,3,64]{0,2,1:T(8,128)(2,1)}, bf16[1024,3,64]{0,2,1:T(8,128)(2,1)S(1)}, u32[]{:S(2)}) copy-start(bf16[1024,3,64]{0,2,1:T(8,128)(2,1)S(1)} %get-tuple-element.2339) | copy-start | bytes 1179652
  484.3 27.0 %copy-start.26 = (bf16[2,512,3,64]{1,3,2,0:T(8,128)(2,1)}, bf16[2,512,3,64]{1,3,2,0:T(8,128)(2,1)S(1)}, u32[]{:S(2)}) copy-start(bf16[2,512,3,64]{1,3,2,0:T(8,128)(2,1)S(1)} %get-tuple-element.2342) | copy-start | bytes 1179652
  517.5 104.6 %reduce-scatter.11.cloned.1.call-start = ((), (), s32[]{:S(2)}) async-start(), calls=%async_computation.28 | async-start | bytes 3932160 | tf_op jit(solution)/shard_map/reduce_scatter | solution.py:58
  562.5 60.8 %copy-start.117 = (f32[768]{0:T(1024)S(1)}, f32[768]{0:T(1024)}, u32[]{:S(2)}) copy-start(f32[768]{0:T(1024)} %get-tuple-element.1129) | copy-start | bytes 9220
  562.5 61.8 %copy-start.137 = (s32[4,64]{1,0:T(4,128)S(1)}, s32[4,64]{1,0:T(4,128)}, u32[]{:S(2)}) copy-start(s32[4,64]{1,0:T(4,128)} %param.47) | copy-start | bytes 3076
  562.5 74.1 %copy-start.138 = (s32[4,64]{1,0:T(4,128)S(1)}, s32[4,64]{1,0:T(4,128)}, u32[]{:S(2)}) copy-start(s32[4,64]{1,0:T(4,128)} %param.48) | copy-start | bytes 3076
  562.6 99.0 %all-gather.17.cloned.1.call-start = ((), (), s32[]{:S(2)}) async-start(), calls=%async_computation.29 | async-start | bytes 1966080 | tf_op jit(solution)/shard_map/all_gather | solution.py:54
  624.3 331.0 %reduce-scatter.13.cloned.1.call-start = ((), (), s32[]{:S(2)}) async-start(), calls=%async_computation.30 | async-start | bytes 3932160 | tf_op jit(solution)/shard_map/reduce_scatter | solution.py:58
  895.8 100.0 %all-gather.19.cloned.1.call-start = ((), (), s32[]{:S(2)}) async-start(), calls=%async_computation.31 | async-start | bytes 1966080 | tf_op jit(solution)/shard_map/all_gather | solution.py:54
  958.7 104.0 %reduce-scatter.15.cloned.1.call-start = ((), (), s32[]{:S(2)}) async-start(), calls=%async_computation.32 | async-start | bytes 3932160 | tf_op jit(solution)/shard_map/reduce_scatter | solution.py:58
  1066.8 27.4 %copy-start.23 = (bf16[1024,3,64]{0,2,1:T(8,128)(2,1)S(1)}, bf16[1024,3,64]{0,2,1:T(8,128)(2,1)}, u32[]{:S(2)}) copy-start(bf16[1024,3,64]{0,2,1:T(8,128)(2,1)} %copy-done.22) | copy-start | bytes 1179652
  1066.8 27.4 %copy-start.77 = (f32[2,3,512,1]{2,1,3,0:T(4,128)S(1)}, f32[2,3,512,1]{2,1,3,0:T(4,128)}, u32[]{:S(2)}) copy-start(f32[2,3,512,1]{2,1,3,0:T(4,128)} %copy-done.76) | copy-start | bytes 36868
  1067.8 20.3 %all-to-all-start.9 = ((bf16[16,64,192]{2,1,0:T(8,128)(2,1)}), bf16[16,64,192]{2,1,0:T(8,128)(2,1)}, u32[]{:S(2)}, u32[]{:S(2)}) async-start(bf16[16,64,192]{2,1,0:T(8,128)(2,1)} %bitcast.165), calls=%async_computation.14 | async-start | bytes 1048576 | tf_op jit(solution)/shard_map/all_to_all | solution.py:281
  1072.4 125.1 %all-gather.21.cloned.1.call-start = ((), (), s32[]{:S(2)}) async-start(), calls=%async_computation.33 | async-start | bytes 1966080 | tf_op jit(solution)/shard_map/all_gather | solution.py:54
  1127.0 31.3 %copy-start.55 = (bf16[1,2,768,768]{2,3,1,0:T(8,128)(2,1)S(1)}, bf16[1,2,768,768]{2,3,1,0:T(8,128)(2,1)}, u32[]{:S(2)}) copy-start(bf16[1,2,768,768]{2,3,1,0:T(8,128)(2,1)} %copy.486) | copy-start | bytes 7077892
  1161.7 123.9 %reduce-scatter.17.cloned.1.call-start = ((), (), s32[]{:S(2)}) async-start(), calls=%async_computation.34 | async-start | bytes 3932160 | tf_op jit(solution)/shard_map/reduce_scatter | solution.py:58
  1208.7 38.0 %copy-start.45 = (bf16[1,1,768,768]{2,3,1,0:T(8,128)(2,1)S(1)}, bf16[1,1,768,768]{2,3,1,0:T(8,128)(2,1)}, u32[]{:S(2)}) copy-start(bf16[1,1,768,768]{2,3,1,0:T(8,128)(2,1)} %copy.462) | copy-start | bytes 3538948
  1214.5 33.0 %copy-start.86 = (bf16[8,4,192]{2,1,0:T(4,128)(2,1)S(1)}, bf16[8,4,192]{2,1,0:T(4,128)(2,1)}, u32[]{:S(2)}) copy-start(bf16[8,4,192]{2,1,0:T(4,128)(2,1)} %copy-done.85) | copy-start | bytes 36868
  1249.8 35.8 %copy-start.107 = (f32[768]{0:T(1024)S(1)}, f32[768]{0:T(1024)}, u32[]{:S(2)}) copy-start(f32[768]{0:T(1024)} %copy-done.106) | copy-start | bytes 9220
  1249.8 37.3 %copy-start.128 = (f32[4,64]{1,0:T(4,128)S(1)}, f32[4,64]{1,0:T(4,128)}, u32[]{:S(2)}) copy-start(f32[4,64]{1,0:T(4,128)} %copy-done.127) | copy-start | bytes 3076
  1249.8 37.4 %copy-start.123 = (f32[4,64]{1,0:T(4,128)S(1)}, f32[4,64]{1,0:T(4,128)}, u32[]{:S(2)}) copy-start(f32[4,64]{1,0:T(4,128)} %copy-done.122) | copy-start | bytes 3076
  1250.6 31.6 %all-to-all-start.15 = ((bf16[16,64,192]{2,1,0:T(8,128)(2,1)}), bf16[16,64,192]{2,1,0:T(8,128)(2,1)S(1)}, u32[]{:S(2)}, u32[]{:S(2)}) async-start(bf16[16,64,192]{2,1,0:T(8,128)(2,1)} %bitcast.206), calls=%async_computation.21 | async-start | bytes 1048576 | tf_op jit(solution)/shard_map/all_to_all | solution.py:281
  1291.1 50.2 %all-to-all-start.11 = ((bf16[16,64,192]{2,1,0:T(8,128)(2,1)}), bf16[16,64,192]{2,1,0:T(8,128)(2,1)}, u32[]{:S(2)}, u32[]{:S(2)}) async-start(bf16[16,64,192]{2,1,0:T(8,128)(2,1)} %bitcast.1074), calls=%async_computation.17 | async-start | bytes 1048576 | tf_op jit(solution)/shard_map/all_to_all | solution.py:281
  1341.3 18.9 %all-to-all-start.16 = ((bf16[16,2,6144]{2,1,0:T(2,128)(2,1)}), bf16[16,2,6144]{2,1,0:T(2,128)(2,1)}, u32[]{:S(2)}, u32[]{:S(2)}) async-start(bf16[16,2,6144]{2,1,0:T(2,128)(2,1)} %reshape.1386), calls=%async_computation.22 | async-start | bytes 786432 | tf_op jit(solution)/shard_map/all_to_all | solution.py:305
  1360.2 47.1 %all-to-all-start.17 = ((bf16[1,1024,2,192]{3,2,0,1:T(2,128)(2,1)}), bf16[1,1024,2,192]{3,2,0,1:T(2,128)(2,1)}, u32[]{:S(2)}, u32[]{:S(2)}) async-start(bf16[1,1024,2,192]{3,2,0,1:T(2,128)(2,1)} %copy.528), calls=%async_computation.23 | async-start | bytes 2097152 | tf_op jit(solution)/shard_map/all_to_all | solution.py:306
  1407.3 18.9 %all-to-all-start.12 = ((bf16[16,2,6144]{2,1,0:T(2,128)(2,1)}), bf16[16,2,6144]{2,1,0:T(2,128)(2,1)}, u32[]{:S(2)}, u32[]{:S(2)}) async-start(bf16[16,2,6144]{2,1,0:T(2,128)(2,1)} %reshape.1382), calls=%async_computation.18 | async-start | bytes 786432 | tf_op jit(solution)/shard_map/all_to_all | solution.py:305
  1413.4 18.2 %copy-start.136 = (f32[256]{0:T(256)S(1)}, f32[256]{0:T(256)}, u32[]{:S(2)}) copy-start(f32[256]{0:T(256)} %copy-done.135) | copy-start | bytes 3076
  1413.5 18.9 %copy-start.48 = (bf16[1,1024,1,192]{3,1,0,2:T(8,128)(2,1)S(1)}, bf16[1,1024,1,192]{3,1,0,2:T(8,128)(2,1)}, u32[]{:S(2)}) copy-start(bf16[1,1024,1,192]{3,1,0,2:T(8,128)(2,1)} %copy-done.47) | copy-start | bytes 1179652
  1413.6 20.4 %copy-start.56 = (bf16[4,192,4,64]{1,3,2,0:T(8,128)(2,1)S(1)}, bf16[4,192,4,64]{1,3,2,0:T(8,128)(2,1)}, u32[]{:S(2)}) copy-start(bf16[4,192,4,64]{1,3,2,0:T(8,128)(2,1)} %get-tuple-element.1373) | copy-start | bytes 1179652
  1426.2 31.2 %all-to-all-start.13 = ((bf16[1,1024,2,192]{3,2,0,1:T(2,128)(2,1)}), bf16[1,1024,2,192]{3,2,0,1:T(2,128)(2,1)}, u32[]{:S(2)}, u32[]{:S(2)}) async-start(bf16[1,1024,2,192]{3,2,0,1:T(2,128)(2,1)} %copy.515), calls=%async_computation.19 | async-start | bytes 2097152 | tf_op jit(solution)/shard_map/all_to_all | solution.py:306
  1430.5 177.1 %all-reduce.4.cloned.1.call-start = ((), (), s32[]{:S(2)}) async-start(), calls=%async_computation.35 | async-start | bytes 589824 | tf_op jit(solution)/shard_map/psum | solution.py:618
  1431.7 20.5 %copy-start.126 = (f32[4,64]{1,0:T(4,128)}, f32[4,64]{1,0:T(4,128)S(1)}, u32[]{:S(2)}) copy-start(f32[4,64]{1,0:T(4,128)S(1)} %rsqrt.86) | copy-start | bytes 3076
  1469.7 138.0 %copy-start.66 = (f32[6,8,768]{2,1,0:T(8,128)S(1)}, f32[6,8,768]{2,1,0:T(8,128)}, u32[]{:S(2)}) copy-start(f32[6,8,768]{2,1,0:T(8,128)} %param.58) | copy-start | bytes 442372
  1469.7 138.0 %copy-start.87 = (f32[6,8,768]{2,1,0:T(8,128)S(1)}, f32[6,8,768]{2,1,0:T(8,128)}, u32[]{:S(2)}) copy-start(f32[6,8,768]{2,1,0:T(8,128)} %param.62) | copy-start | bytes 442372
  1469.7 138.0 %copy-start.88 = (f32[6,8,768]{2,1,0:T(8,128)S(1)}, f32[6,8,768]{2,1,0:T(8,128)}, u32[]{:S(2)}) copy-start(f32[6,8,768]{2,1,0:T(8,128)} %param.61) | copy-start | bytes 442372
  1471.3 139.4 %copy-start.89 = (f32[6,8,768]{2,1,0:T(8,128)S(1)}, f32[6,8,768]{2,1,0:T(8,128)}, u32[]{:S(2)}) copy-start(f32[6,8,768]{2,1,0:T(8,128)} %param.60) | copy-start | bytes 442372
  1471.3 139.4 %copy-start.90 = (f32[6,8,768]{2,1,0:T(8,128)S(1)}, f32[6,8,768]{2,1,0:T(8,128)}, u32[]{:S(2)}) copy-start(f32[6,8,768]{2,1,0:T(8,128)} %param.59) | copy-start | bytes 442372
  (119 other events, 729.5 us)
Sparse Core Ops, SparseCore 0:
  62.0 109.3 reduce-scatter.6
  283.7 59.4 all-gather.12
  358.0 64.5 reduce-scatter.8
  517.6 35.7 all-gather.14
  562.7 59.2 reduce-scatter.10
  624.4 37.0 all-gather.16
  895.9 59.3 reduce-scatter.12
  958.9 36.9 all-gather.18
  1003.4 59.2 reduce-scatter.14
  1161.8 35.7 all-gather.20
  1205.1 73.8 reduce-scatter.16
  1481.6 126.0 all-reduce.3
where the time goes:
time: 1640 us; the launch traced here: 1620 us
  waiting for transfers between devices  686 us (42%)
  matrix products  311 us (19%)
  local copies, waits for them, and re-layouts  232 us (14%)
  blocking collectives  176 us (11%)
  other arithmetic  115 us (7%)
  starting transfers between devices  78.1 us (5%)
  between operations  21.4 us (1%)
    reduce_scatter x6, waiting for transfers between devices, col_sums(): return lax.psum_scatter(terms, 'col', scatter_dimension=0, tiled=True)  269 us
    psum x1, waiting for transfers between devices, per_device(): lax.psum((down_gradient, up_gradient), ('dp', 'head', 'col'))  123 us
    all_gather x5, waiting for transfers between devices, col_rows(): return lax.all_gather(rows_low, 'col', axis=0, tiled=True)  120 us
    dot_general x4, matrix products, one_block(): return jnp.dot(grad_logits, embedding, preferred_element_type=jnp.float32)  85.6 us
    all_to_all x3, waiting for transfers between devices, attention_forward(): lax.all_to_all(sent_pair, ('head', 'col'), split_axis=0, concat_axis=1, t...  68.1 us
    unnamed x295, local copies, waits for them, and re-layouts  46.6 us
    dot_general x4, matrix products, one_block(): lax.dot_general(rows_blk, embedding, (((1,), (1,)), ((), ())), preferred_...  45.4 us
    all_to_all x3, waiting for transfers between devices, attention_backward(): lax.all_to_all(grad_back.astype(jnp.bfloat16).reshape(n_head * rows_n, pi...  43.4 us
  transfers between devices with their start and end apart: 27, of which 23 were waited for; matrix products, arithmetic and copies ran while one was open for 15% of the time, Pallas kernels for 0%

commit v1 on v0

v1 whole, which is shorter than its diff:
```python
import jax
import jax.numpy as jnp
from jax import lax
from jax.sharding import PartitionSpec as P

MODEL_DIMENSION = 768
HEAD_DIM = 64
ADAPTER_RANK = 8
LEN = 1024


ADAPTER_SCALE = 2.0
ORTH_WEIGHT = 0.2
BASE_NORM_WEIGHT = 0.02
DOWN_STEP_RATE = 0.05
UP_STEP_RATE = 0.2
BETA_ONE = 0.9
BETA_TWO = 0.999
ADAM_EPS = 1e-08
DECAY = 0.01
NEG_FILL = -1e30


def swapped(x, axis, step):
    return lax.ppermute(x, axis, [(i, i ^ step) for i in range(lax.axis_size(axis))])


def summed(x, axes):
    for axis in axes:
        step = 1
        while step < lax.axis_size(axis):
            x = jax.tree.map(lambda part: part + swapped(part, axis, step), x)
            step *= 2
    return x


def collected(x, axis):
    n = lax.axis_size(axis)
    me = lax.axis_index(axis)
    parts = jnp.stack([x] + [swapped(x, axis, step) for step in range(1, n)])
    return jnp.stack(
        [lax.dynamic_index_in_dim(parts, me ^ at, 0, keepdims=False) for at in range(n)]
    )


def scattered_sum(x, axis):
    n = lax.axis_size(axis)
    me = lax.axis_index(axis)
    total = lax.dynamic_index_in_dim(x, me, 0, keepdims=False)
    for step in range(1, n):
        block = lax.dynamic_index_in_dim(x, me ^ step, 0, keepdims=False)
        total = total + swapped(block, axis, step)
    return total


def rms_norm(values, gain_row):
    return values * lax.rsqrt(jnp.mean(values * values, axis=-1, keepdims=True) + 1e-06) * gain_row


def norm_back(values, gain_row, grad_out, scale_by):
    primal, backward_function = jax.vjp(
        lambda inner_vals: rms_norm(inner_vals, gain_row) * scale_by, values
    )
    return backward_function(grad_out)[0]


def segment_of(lengths, length_total):
    bounds = jnp.cumsum(lengths, dtype=jnp.int32)
    places = jnp.arange(length_total, dtype=jnp.int32)
    return jnp.sum(
        (places[:, None] >= bounds[None, :-1]).astype(jnp.int32), axis=1, dtype=jnp.int32
    )


def col_rows(rows_low):
    return lax.all_gather(rows_low, "col", axis=0, tiled=True)


def col_sums(terms):
    return lax.psum_scatter(terms, "col", scatter_dimension=0, tiled=True)


def head_trade(blocks):
    return lax.all_to_all(blocks, "head", split_axis=0, concat_axis=0, tiled=True)


def score_block(q_block, key_rows, seg_block, seg_key, start_at, causal):
    scores = jnp.einsum(
        "qhd,khd->hqk", q_block, key_rows, preferred_element_type=jnp.float32
    ) * HEAD_DIM ** (-0.5)
    allowed = seg_block[:, None] == seg_key[None, :]
    if causal:
        query_at = start_at + jnp.arange(q_block.shape[0], dtype=jnp.int32)
        key_at = jnp.arange(seg_key.shape[0], dtype=jnp.int32)
        allowed = allowed & (key_at[None, :] <= query_at[:, None])
    return jnp.where(allowed[None], scores, NEG_FILL)


def attend_forward(queries, key_rows, value_rows, seg_query, seg_key, causal):
    length_q, heads_here, head_width = queries.shape
    block_rows = min(512, length_q)
    blocks = length_q // block_rows

    def one_block(members):
        q_block, seg_block, start_at = members
        scores = score_block(q_block, key_rows, seg_block, seg_key, start_at, causal)
        row_top = jnp.max(scores, axis=2, keepdims=True)
        exponent = jnp.exp(scores - row_top)
        row_total = jnp.sum(exponent, axis=2, keepdims=True)
        probs_low = (exponent / row_total).astype(jnp.bfloat16)
        mixed_heads = jnp.einsum(
            "hqk,khd->qhd", probs_low, value_rows, preferred_element_type=jnp.float32
        )
        return (mixed_heads.astype(jnp.bfloat16), row_top, row_total)

    starts = jnp.arange(blocks, dtype=jnp.int32) * block_rows
    mixed_heads, row_tops, row_sums = lax.map(
        one_block,
        (
            queries.reshape(blocks, block_rows, heads_here, head_width),
            seg_query.reshape(blocks, block_rows),
            starts,
        ),
    )
    return (mixed_heads.reshape(length_q, heads_here, head_width), row_tops, row_sums)


def attend_backward(
    queries, key_rows, value_rows, seg_query, seg_key, causal, row_tops, row_sums, grad_mixed, want_keys
):
    length_q, heads_here, head_width = queries.shape
    block_rows = min(512, length_q)
    blocks = length_q // block_rows
    score_scale = HEAD_DIM ** (-0.5)

    def one_block(carried, members):
        grad_keys, grad_values = carried
        q_block, seg_block, start_at, top_block, total_block, grad_block = members
        scores = score_block(q_block, key_rows, seg_block, seg_key, start_at, causal)
        probs_f = jnp.exp(scores - top_block) / total_block
        grad_probs = jnp.einsum(
            "qhd,khd->hqk", grad_block, value_rows, preferred_element_type=jnp.float32
        )
        inner_sum = jnp.sum(grad_probs * probs_f, axis=2, keepdims=True)
        grad_scores = (probs_f * (grad_probs - inner_sum)).astype(jnp.bfloat16)
        grad_q = (
            jnp.einsum("hqk,khd->qhd", grad_scores, key_rows, preferred_element_type=jnp.float32)
            * score_scale
        )
        if want_keys:
            grad_keys = (
                grad_keys
                + jnp.einsum(
                    "hqk,qhd->khd", grad_scores, q_block, preferred_element_type=jnp.float32
                )
                * score_scale
            )
        grad_values = grad_values + jnp.einsum(
            "hqk,qhd->khd",
            probs_f.astype(jnp.bfloat16),
            grad_block,
            preferred_element_type=jnp.float32,
        )
        return ((grad_keys, grad_values), grad_q)

    empty_kv = jnp.zeros(key_rows.shape, jnp.float32)
    starts = jnp.arange(blocks, dtype=jnp.int32) * block_rows
    members = (
        queries.reshape(blocks, block_rows, heads_here, head_width),
        seg_query.reshape(blocks, block_rows),
        starts,
        row_tops,
        row_sums,
        grad_mixed.reshape(blocks, block_rows, heads_here, head_width),
    )
    (grad_keys, grad_values), grad_q = lax.scan(one_block, (empty_kv, empty_kv), members)
    return (grad_q.reshape(length_q, heads_here, head_width), grad_keys, grad_values)


def contract(left, right, left_dim, right_dim):
    return lax.dot_general(
        left, right, (((left_dim,), (right_dim,)), ((), ())), preferred_element_type=jnp.float32
    )


def adapter_forward(normed_input, down_one, up_one):
    inner_low = contract(normed_input, down_one, 1, 1).astype(jnp.bfloat16)
    return (inner_low, ADAPTER_SCALE * contract(inner_low, up_one, 1, 0))


def adapter_back(grad_side, inner_low, normed_input, down_one, up_one):
    up_gradient = ADAPTER_SCALE * contract(inner_low, grad_side, 0, 0)
    grad_inner = (ADAPTER_SCALE * contract(grad_side, up_one, 1, 1)).astype(jnp.bfloat16)
    down_gradient = contract(grad_inner, normed_input, 0, 0)
    return (down_gradient, up_gradient, contract(grad_inner, down_one, 1, 0))


def by_head(rows, n_head):
    length, width = rows.shape
    return rows.reshape(length, n_head, width // n_head).transpose(1, 0, 2)


def from_head(blocks):
    n_head, length, width = blocks.shape
    return blocks.transpose(1, 0, 2).reshape(length, n_head * width)


def attention_forward(
    normed_q, normed_kv, qkv_w, out_w, down_pair, up_pair, seg_query, seg_key, causal
):
    n_head = lax.axis_size("head")
    piece_n, model_width = normed_q.shape
    heads_here = model_width // n_head // HEAD_DIM
    inner_q, lifted_q = adapter_forward(normed_q, down_pair[0], up_pair[0])
    inner_v, lifted_v = adapter_forward(normed_kv, down_pair[1], up_pair[1])
    queries = (contract(normed_q, qkv_w[0], 1, 0) + lifted_q).astype(jnp.bfloat16)
    keys = contract(normed_kv, qkv_w[1], 1, 0).astype(jnp.bfloat16)
    values = (contract(normed_kv, qkv_w[2], 1, 0) + lifted_v).astype(jnp.bfloat16)
    got = head_trade(
        jnp.stack([by_head(queries, n_head), by_head(keys, n_head), by_head(values, n_head)], 1)
    )
    queries_a, keys_a, values_a = [
        got[:, kind].reshape(n_head * piece_n, heads_here, HEAD_DIM) for kind in range(3)
    ]
    mixed_heads, row_tops, row_sums = attend_forward(
        queries_a, keys_a, values_a, seg_query, seg_key, causal
    )
    back_rows = from_head(head_trade(mixed_heads.reshape(n_head, piece_n, -1)))
    result = contract(back_rows, out_w, 1, 0)
    return (result, (inner_q, inner_v, queries_a, keys_a, values_a, row_tops, row_sums))


def attention_backward(
    grad_res,
    normed_q,
    normed_kv,
    kept_fwd,
    qkv_w,
    out_w,
    down_pair,
    up_pair,
    seg_query,
    seg_key,
    causal,
    want_inputs,
):
    inner_q, inner_v, queries_a, keys_a, values_a, row_tops, row_sums = kept_fwd
    n_head = lax.axis_size("head")
    head_at = lax.axis_index("head")
    piece_n, model_width = normed_q.shape
    group_w = model_width // n_head
    heads_here = group_w // HEAD_DIM
    grad_back = contract(grad_res.astype(jnp.bfloat16), out_w, 1, 1).astype(jnp.bfloat16)
    grad_mixed = head_trade(by_head(grad_back, n_head))
    grad_q, grad_k, grad_v = attend_backward(
        queries_a,
        keys_a,
        values_a,
        seg_query,
        seg_key,
        causal,
        row_tops,
        row_sums,
        grad_mixed.reshape(n_head * piece_n, heads_here, HEAD_DIM),
        want_inputs,
    )
    grad_q, grad_k, grad_v = [
        part.astype(jnp.bfloat16).reshape(n_head * piece_n, group_w)
        for part in (grad_q, grad_k, grad_v)
    ]
    if not want_inputs:
        inner_both = jnp.concatenate([inner_q, inner_v], axis=1).T
        inner_all = collected(inner_both, "head").transpose(1, 0, 2).reshape(
            2 * ADAPTER_RANK, n_head * piece_n
        )
        partial_inner = []
        up_gradients = []
        for at, grad_side in enumerate((grad_q, grad_v)):
            up_here = lax.dynamic_slice_in_dim(up_pair[at], head_at * group_w, group_w, 1)
            partial_inner.append(contract(up_here, grad_side, 1, 1))
            up_gradients.append(
                lax.dynamic_update_slice_in_dim(
                    jnp.zeros((ADAPTER_RANK, model_width), jnp.float32),
                    ADAPTER_SCALE
                    * contract(
                        inner_all[at * ADAPTER_RANK : (at + 1) * ADAPTER_RANK], grad_side, 1, 0
                    ),
                    head_at * group_w,
                    1,
                )
            )
        partial_inner = jnp.concatenate(partial_inner, axis=0)
        own_inner = scattered_sum(
            partial_inner.reshape(2 * ADAPTER_RANK, n_head, piece_n).transpose(1, 0, 2), "head"
        )
        own_inner = (ADAPTER_SCALE * own_inner).astype(jnp.bfloat16)
        return (
            None,
            None,
            (
                contract(own_inner[:ADAPTER_RANK], normed_q, 1, 0),
                contract(own_inner[ADAPTER_RANK:], normed_kv, 1, 0),
            ),
            tuple(up_gradients),
        )
    got = head_trade(
        jnp.stack([part.reshape(n_head, piece_n, group_w) for part in (grad_q, grad_k, grad_v)], 1)
    )
    grad_qt, grad_kt, grad_vt = [from_head(got[:, kind]) for kind in range(3)]
    down_query, up_query, side_q = adapter_back(
        grad_qt, inner_q, normed_q, down_pair[0], up_pair[0]
    )
    down_value, up_value, side_v = adapter_back(
        grad_vt, inner_v, normed_kv, down_pair[1], up_pair[1]
    )
    normed_query_gradient = contract(grad_qt, qkv_w[0], 1, 1) + side_q
    normed_key_value_gradient = (
        contract(grad_kt, qkv_w[1], 1, 1) + contract(grad_vt, qkv_w[2], 1, 1) + side_v
    )
    return (
        normed_query_gradient,
        normed_key_value_gradient,
        (down_query, down_value),
        (up_query, up_value),
    )


def whole_ffn(weight_pair):
    copies = lax.axis_size("dp") * lax.axis_size("head")
    copy_at = lax.axis_index("dp") * lax.axis_size("head") + lax.axis_index("head")
    units = weight_pair.shape[1] // copies
    share = lax.dynamic_slice_in_dim(weight_pair, copy_at * units, units, 1)
    share = jnp.concatenate([share[0], share[1]], axis=1)
    return lax.all_gather(share, ("dp", "head", "col"), axis=0, tiled=True)


def ffn_forward(normed_input, units):
    model_width = normed_input.shape[-1]
    pre_act = contract(normed_input, units[:, :model_width], 1, 1)
    hidden = jnp.maximum(pre_act, 0.0).astype(jnp.bfloat16)
    return (contract(hidden, units[:, model_width:], 1, 0), pre_act > 0.0)


def ffn_backward(grad_res, active, units):
    model_width = grad_res.shape[-1]
    grad_hidden = contract(grad_res.astype(jnp.bfloat16), units[:, model_width:], 1, 1)
    grad_pre = jnp.where(active, grad_hidden, 0.0).astype(jnp.bfloat16)
    return contract(grad_pre, units[:, :model_width], 1, 0)


def vocab_stats(head_rows, clipped, inside, embedding, n_col):
    model_width = head_rows.shape[1]

    def one_block(members):
        rows_blk, clip_blk, inside_blk = members
        logits = lax.dot_general(
            rows_blk, embedding, (((1,), (1,)), ((), ())), preferred_element_type=jnp.float32
        )
        row_top = jnp.max(logits, axis=1)
        row_total = jnp.sum(jnp.exp(logits - row_top[:, None]), axis=1)
        picked = jnp.take_along_axis(logits, clip_blk[:, None], axis=1)[:, 0]
        return (row_top, row_total, jnp.where(inside_blk, picked, 0.0))

    block_outs = lax.map(
        one_block,
        (
            head_rows.reshape(n_col, -1, model_width),
            clipped.reshape(n_col, -1),
            inside.reshape(n_col, -1),
        ),
    )
    return tuple((member.reshape(-1) for member in block_outs))


def vocab_back(head_rows, clipped, inside, embedding, n_col, log_total, coef_rows):
    model_width = head_rows.shape[1]
    vocab_part = embedding.shape[0]

    def one_block(members):
        rows_blk, clip_blk, inside_blk, total_blk, coef_blk = members
        logits = lax.dot_general(
            rows_blk, embedding, (((1,), (1,)), ((), ())), preferred_element_type=jnp.float32
        )
        probs_f = jnp.exp(logits - total_blk[:, None])
        hits = (jnp.arange(vocab_part, dtype=jnp.int32)[None, :] == clip_blk[:, None]) & inside_blk[
            :, None
        ]
        grad_logits = (coef_blk[:, None] * (probs_f - hits.astype(jnp.float32))).astype(
            jnp.bfloat16
        )
        return jnp.dot(grad_logits, embedding, preferred_element_type=jnp.float32)

    members = (
        head_rows.reshape(n_col, -1, model_width),
        clipped.reshape(n_col, -1),
        inside.reshape(n_col, -1),
        log_total.reshape(n_col, -1),
        coef_rows.reshape(n_col, -1),
    )
    return lax.map(one_block, members).reshape(-1, model_width)


def merge_stats(left_side, right_side):
    top_both = jnp.maximum(left_side[0], right_side[0])
    summed = left_side[1] * jnp.exp(left_side[0] - top_both) + right_side[1] * jnp.exp(
        right_side[0] - top_both
    )
    return (top_both, summed, left_side[2] + right_side[2])


def adam_update(weights, gradient, first_moment, second_moment, step_rate, step_count_float):
    first_new = BETA_ONE * first_moment + (1.0 - BETA_ONE) * gradient
    second_new = BETA_TWO * second_moment + (1.0 - BETA_TWO) * gradient * gradient
    first_hat = first_new / (1.0 - BETA_ONE**step_count_float)
    second_hat = second_new / (1.0 - BETA_TWO**step_count_float)
    weights_new = weights - step_rate * (
        first_hat / (jnp.sqrt(second_hat) + ADAM_EPS) + DECAY * weights
    )
    return (weights_new, first_new, second_new)


def per_device(
    encoder_token_ids,
    decoder_token_ids,
    target_token_ids,
    target_count_mask,
    encoder_document_length,
    decoder_document_length,
    embedding,
    attention_projection_weight,
    attention_output_weight,
    feedforward_weight,
    norm_gain_rows,
    earlier_down_weight,
    adapter_down_weight,
    adapter_up_weight,
    down_first_moment,
    down_second_moment,
    up_first_moment,
    up_second_moment,
    optimizer_step_count,
):
    n_col = lax.axis_size("col")
    col_at = lax.axis_index("col")
    vocab_part, model_width = embedding.shape
    tables = jnp.stack(
        [encoder_token_ids, decoder_token_ids, target_token_ids, target_count_mask]
    )
    tables = collected(tables, "col").transpose(1, 2, 0, 3)
    enc_all, dec_all, target_all, mask_all = tables.reshape(4, -1)

    def lookup(ids_flat):
        local_ids = ids_flat - col_at * vocab_part
        inside_ids = (local_ids >= 0) & (local_ids < vocab_part)
        picked = jnp.take(embedding, jnp.clip(local_ids, 0, vocab_part - 1), axis=0)
        return col_sums(
            jnp.where(inside_ids[:, None], picked, jnp.zeros((), picked.dtype))
        ).astype(jnp.float32)

    enc_state = lookup(enc_all)
    units_enc = whole_ffn(feedforward_weight[0])
    dec_state = lookup(dec_all)
    units_dec = whole_ffn(feedforward_weight[1])
    mask_float = mask_all.astype(jnp.float32)
    target_count = summed(jnp.sum(mask_float), ("dp", "head"))
    down_low_rank = adapter_down_weight.astype(jnp.bfloat16)
    up_low_rank = adapter_up_weight.astype(jnp.bfloat16)
    enc_seg = segment_of(
        lax.dynamic_index_in_dim(encoder_document_length, col_at, 0, keepdims=False), LEN
    )
    dec_seg = segment_of(
        lax.dynamic_index_in_dim(decoder_document_length, col_at, 0, keepdims=False), LEN
    )

    def weights_of(slot_at):
        return (
            attention_projection_weight[slot_at],
            attention_output_weight[slot_at],
            down_low_rank[2 * slot_at : 2 * slot_at + 2],
            up_low_rank[2 * slot_at : 2 * slot_at + 2],
        )

    enc_normed = rms_norm(enc_state, norm_gain_rows[0]).astype(jnp.bfloat16)
    branch_out, kept_enc = attention_forward(
        enc_normed, enc_normed, *weights_of(0), enc_seg, enc_seg, False
    )
    enc_mid = enc_state + branch_out
    dec_normed = rms_norm(dec_state, norm_gain_rows[3]).astype(jnp.bfloat16)
    branch_out, kept_self = attention_forward(
        dec_normed, dec_normed, *weights_of(1), dec_seg, dec_seg, True
    )
    dec_one = dec_state + branch_out
    branch_out, active_enc = ffn_forward(
        rms_norm(enc_mid, norm_gain_rows[1]).astype(jnp.bfloat16), units_enc
    )
    enc_last = enc_mid + branch_out
    encoded = rms_norm(enc_last, norm_gain_rows[2]).astype(jnp.bfloat16)
    cross_normed = rms_norm(dec_one, norm_gain_rows[4]).astype(jnp.bfloat16)
    branch_out, kept_cross = attention_forward(
        cross_normed, encoded, *weights_of(2), dec_seg, enc_seg, False
    )
    dec_two = dec_one + branch_out
    branch_out, active_dec = ffn_forward(
        rms_norm(dec_two, norm_gain_rows[5]).astype(jnp.bfloat16), units_dec
    )
    dec_three = dec_two + branch_out
    head_scale = MODEL_DIMENSION ** (-0.5)
    final_rows = (rms_norm(dec_three, norm_gain_rows[6]) * head_scale).astype(jnp.bfloat16)
    head_rows = col_rows(final_rows)
    local_t = target_all - col_at * vocab_part
    inside = (local_t >= 0) & (local_t < vocab_part)
    clipped = jnp.clip(local_t, 0, vocab_part - 1)
    stats = vocab_stats(head_rows, clipped, inside, embedding, n_col)
    step = 1
    while step < n_col:
        others = swapped(jnp.stack(stats), "col", step)
        stats = merge_stats(stats, (others[0], others[1], others[2]))
        step *= 2
    row_top, row_total, row_target = stats
    log_total = row_top + jnp.log(row_total)
    ce_local = jnp.sum(mask_float * (log_total - row_target))
    ce_total = summed(ce_local, ("dp", "head"))
    grad_rows = vocab_back(
        head_rows, clipped, inside, embedding, n_col, log_total, mask_float / target_count
    )
    grad_final = col_sums(grad_rows)
    grad_dec = norm_back(dec_three, norm_gain_rows[6], grad_final, head_scale)
    grad_dec = grad_dec + norm_back(
        dec_two, norm_gain_rows[5], ffn_backward(grad_dec, active_dec, units_dec), 1.0
    )
    normed_query_gradient, grad_encoded, downs_cross, ups_cross = attention_backward(
        grad_dec, cross_normed, encoded, kept_cross, *weights_of(2), dec_seg, enc_seg, False, True
    )
    cross_sums = summed(jnp.stack(downs_cross + ups_cross), ("head", "dp", "col"))
    grad_dec = grad_dec + norm_back(dec_one, norm_gain_rows[4], normed_query_gradient, 1.0)
    unused_q, unused_kv, downs_self, ups_self = attention_backward(
        grad_dec, dec_normed, dec_normed, kept_self, *weights_of(1), dec_seg, dec_seg, True, False
    )
    grad_enc = norm_back(enc_last, norm_gain_rows[2], grad_encoded, 1.0)
    grad_enc = grad_enc + norm_back(
        enc_mid, norm_gain_rows[1], ffn_backward(grad_enc, active_enc, units_enc), 1.0
    )
    unused_q, unused_kv, downs_enc, ups_enc = attention_backward(
        grad_enc, enc_normed, enc_normed, kept_enc, *weights_of(0), enc_seg, enc_seg, False, False
    )
    self_sums = summed(
        jnp.stack(downs_enc + downs_self + ups_enc + ups_self), ("head", "dp", "col")
    )
    down_penalty_sum = jnp.concatenate([self_sums[:4], cross_sums[:2]])
    up_penalty_sum = jnp.concatenate([self_sums[4:], cross_sums[2:]])
    earlier_down_float = earlier_down_weight.astype(jnp.float32)
    intersection = jnp.einsum(
        "hygm,hvm->hygv", earlier_down_float, adapter_down_weight, precision=lax.Precision.HIGHEST
    )
    penalty = ORTH_WEIGHT * jnp.sum(intersection * intersection) + BASE_NORM_WEIGHT * jnp.sum(
        adapter_up_weight * adapter_up_weight
    )
    down_penalty_sum = down_penalty_sum + 2.0 * ORTH_WEIGHT * jnp.einsum(
        "aoij,aoid->ajd", intersection, earlier_down_float, precision=lax.Precision.HIGHEST
    )
    up_penalty_sum = up_penalty_sum + 2.0 * BASE_NORM_WEIGHT * adapter_up_weight
    loss_scalar = ce_total / target_count + penalty
    step_count_float = optimizer_step_count[0].astype(jnp.float32)
    updated_down_weight, down_first_updated, down_second_updated = adam_update(
        adapter_down_weight,
        down_penalty_sum,
        down_first_moment,
        down_second_moment,
        DOWN_STEP_RATE,
        step_count_float,
    )
    updated_up_weight, up_first_updated, up_second_updated = adam_update(
        adapter_up_weight,
        up_penalty_sum,
        up_first_moment,
        up_second_moment,
        UP_STEP_RATE,
        step_count_float,
    )
    return (
        loss_scalar,
        updated_down_weight,
        down_first_updated,
        down_second_updated,
        updated_up_weight,
        up_first_updated,
        up_second_updated,
    )


def solution(mesh):
    in_specs = (
        P("dp", ("head", "col")),
        P("dp", ("head", "col")),
        P("dp", ("head", "col")),
        P("dp", ("head", "col")),
        P("dp", None),
        P("dp", None),
        P("col", None),
        P(),
        P(),
        P(None, None, "col", None),
        P(),
        P(),
        P(),
        P(),
        P(),
        P(),
        P(),
        P(),
        P(),
    )
    out_specs = (P(), P(), P(), P(), P(), P(), P())
    return jax.shard_map(
        per_device, mesh=mesh, in_specs=in_specs, out_specs=out_specs, check_vma=False
    )
```

time: 1640 us -> 882 us (0.54)
  waiting for transfers between devices: 686 us -> 217 us
  blocking collectives: 176 us -> 9.8 us
  local copies, waits for them, and re-layouts: 232 us -> 155 us
  other arithmetic: 115 us -> 67.9 us
    reduce_scatter x6 -> x3, waiting for transfers between devices: 269 us -> 104 us  [col_sums(): return lax.psum_scatter(terms, 'col', scatter_dimension=0, tiled=True)]
    all_to_all x15 -> x9, waiting for transfers between devices: 175 us -> 37 us  [head_trade(): lax.all_to_all(blocks, 'head', split_axis=0, concat_axis=0, tiled=True)]
    psum x1 -> x0, waiting for transfers between devices: 123 us -> none  [per_device(): lax.psum((down_gradient, up_gradient), ('dp', 'head', 'col'))]
    all_gather x7 -> x0, blocking collectives: 90 us -> none  [the longest x3 39.6 us: joined(): everything = jax.tree.map(lambda part: lax.all_gather(part, axis), x)]
    all_gather x5 -> x1, waiting for transfers between devices: 120 us -> 36.7 us  [col_rows(): return lax.all_gather(rows_low, 'col', axis=0, tiled=True)]
    all_to_all x3 -> x1, blocking collectives: 73.7 us -> 9.8 us  [head_trade(): lax.all_to_all(blocks, 'head', split_axis=0, concat_axis=0, tiled=True)]
    ppermute x0 -> x33, starting transfers between devices: none -> 42.4 us  [swapped(): lax.ppermute(x, axis, [(i, i ^ step) for i in range(lax.axis_size(axis))])]
    ppermute x0 -> x33, waiting for transfers between devices: none -> 38.7 us  [swapped(): lax.ppermute(x, axis, [(i, i ^ step) for i in range(lax.axis_size(axis))])]
  transfers between devices with their start and end apart: 27 -> 48, of which waited for: 23 -> 24; matrix products, arithmetic and copies ran while one was open for 15% -> 30% of each run, Pallas kernels for 0% -> 0%
where the time goes in v1:
time: 882 us; the launch traced here: 870 us
  matrix products  313 us (35%)
  waiting for transfers between devices  217 us (25%)
  local copies, waits for them, and re-layouts  155 us (18%)
  starting transfers between devices  79.4 us (9%)
  other arithmetic  67.9 us (8%)
  between operations  26.1 us (3%)
  blocking collectives  9.8 us (1%)
    reduce_scatter x3, waiting for transfers between devices, col_sums(): return lax.psum_scatter(terms, 'col', scatter_dimension=0, tiled=True)  104 us
    dot_general x56, matrix products, contract(): lax.dot_general(left, right, (((left_dim,), (right_dim,)), ((), ())), pre...  95.8 us
    dot_general x4, matrix products, one_block(): return jnp.dot(grad_logits, embedding, preferred_element_type=jnp.float32)  85.7 us
    dot_general x4, matrix products, one_block(): lax.dot_general(rows_blk, embedding, (((1,), (1,)), ((), ())), preferred_...  45.3 us
    ppermute x33, starting transfers between devices, swapped(): lax.ppermute(x, axis, [(i, i ^ step) for i in range(lax.axis_size(axis))])  42.4 us
    ppermute x33, waiting for transfers between devices, swapped(): lax.ppermute(x, axis, [(i, i ^ step) for i in range(lax.axis_size(axis))])  38.7 us
    all_to_all x9, waiting for transfers between devices, head_trade(): lax.all_to_all(blocks, 'head', split_axis=0, concat_axis=0, tiled=True)  37 us
    all_gather x1, waiting for transfers between devices, col_rows(): return lax.all_gather(rows_low, 'col', axis=0, tiled=True)  36.7 us
  transfers between devices with their start and end apart: 48, of which 24 were waited for; matrix products, arithmetic and copies ran while one was open for 30% of the time, Pallas kernels for 0%

profile of v1, /device:TPU:0, one launch (start us, length us, event | category | flops | bytes accessed | tf_op | source)
XLA Modules:
  0.0 870.1 jit_solution(11524666810018558382)
XLA Ops:
  16.5 3.5 collective-permute-done.2
  21.6 10.6 %gather_fusion.1 = bf16[1024,768]{1,0:T(8,128)(2,1)S(1)} fusion(bf16[8032,768]{1,0:T(8,128)(2,1)} %param.43, s32[1024]{0:T(1024)S(1)} %get-tuple-element.1118), kind=kCustom, calls=%fused_computation.clone | custom fusion | bytes 3149824 | tf_op jit(solution)/shard_map/jit(_take)/gather | solution.py:455
  33.9 10.7 %gather_fusion.2 = bf16[1024,768]{1,0:T(8,128)(2,1)S(1)} fusion(bf16[8032,768]{1,0:T(8,128)(2,1)} %param.43, s32[1024]{0:T(1024)S(1)} %get-tuple-element.1119), kind=kCustom, calls=%fused_computation.2.clone | custom fusion | bytes 3149824 | tf_op jit(solution)/shard_map/jit(_take)/gather | solution.py:455
  53.5 14.9 %reduce-scatter.4.cloned.1.call-done = bf16[256,768]{1,0:T(8,128)(2,1)} async-done(((bf16[1024,768]{1,0:T(8,128)(2,1)}), bf16[256,768]{1,0:T(8,128)(2,1)}) %reduce-scatter.4.cloned.1.call-update) | async-done | bytes 393232 | tf_op jit(solution)/shard_map/reduce_scatter | solution.py:80
  80.2 3.7 all-to-all-start
  83.9 31.5 %reduce-scatter.6.cloned.1.call-done = bf16[256,768]{1,0:T(8,128)(2,1)} async-done(((bf16[1024,768]{1,0:T(8,128)(2,1)}), bf16[256,768]{1,0:T(8,128)(2,1)}) %reduce-scatter.6.cloned.1.call-update) | async-done | bytes 393232 | tf_op jit(solution)/shard_map/reduce_scatter | solution.py:80
  130.0 3.5 all-to-all-start.2
  142.0 18.3 %while.107 = (s32[]{:T(128)}, bf16[2,512,3,64]{1,3,2,0:T(8,128)(2,1)}, f32[2,3,512,1]{2,1,3,0:T(4,128)}, f32[2,3,512,1]{2,1,3,0:T(4,128)}, s32[2,512]{1,0:T(2,12...) while((s32[]{:T(128)}, ...), condition=%wide.region_7.9_spmd, body=%wide.region_4.8_spmd.sunk | while | flops 423196160 | bytes 22226052 | solution.py:117
  166.5 4.3 all-to-all-start.1
  175.7 11.6 %while.108 = (s32[]{:T(128)}, bf16[2,512,3,64]{1,3,2,0:T(8,128)(2,1)S(1)}, f32[2,3,512,1]{2,1,3,0:T(4,128)S(1)}, f32[2,3,512,1]{2,1,3,0:T(4,128)S(1)}, s32[2,512...) while((s32[]{:T(128)}, ...), condition=%wide.region_16.18_spmd, body=%wide.region_13.17_spmd.sunk | while | flops 422147072 | bytes 22229108 | solution.py:117
  189.9 4.1 all-to-all-start.3
  200.1 5.1 all-to-all-done.3
  207.9 3.8 fusion.148
  211.7 4.9 multiply_reduce_fusion.10
  227.0 3.5 all-to-all-start.4
  231.0 17.3 %all-to-all-done.4 = bf16[4,3,256,192]{2,3,1,0:T(8,128)(2,1)S(1)} async-done(((bf16[4,3,256,192]{2,3,1,0:T(8,128)(2,1)}), bf16[4,3,256,192]{2,3,1,0:T(8,128)(2,1)S(1)}, u32[]{:S(2)}, u32[]{:S(2)}) %all-to-all-start.4) | async-done | bytes 1179680 | tf_op jit(solution)/shard_map/all_to_all | solution.py:84
  254.4 12.9 %while.109 = (s32[]{:T(128)}, bf16[2,512,3,64]{1,3,2,0:T(8,128)(2,1)}, f32[2,3,512,1]{2,1,3,0:T(4,128)S(1)}, f32[2,3,512,1]{2,1,3,0:T(4,128)S(1)}, s32[2,512]{1,...) while((s32[]{:T(128)}, ...), condition=%wide.region_22.24_spmd, body=%wide.region_19.23_spmd.sunk | while | flops 422147072 | bytes 22225520 | solution.py:117
  270.9 9.8 %all_to_all.50 = bf16[4,256,192]{1,2,0:T(8,128)(2,1)S(1)} all-to-all(bf16[4,256,192]{1,2,0:T(8,128)(2,1)S(1)} %copy.219), channel_id=1, replica_groups=mesh['dp'=2,'head'=4,'col'=4] {'head'}, dimensions={0} | all-to-all | bytes 786432 | tf_op jit(solution)/shard_map/all_to_all | solution.py:84
  283.9 4.1 fusion.140
  288.1 4.9 multiply_reduce_fusion.8
  295.3 36.7 %all-gather.8.cloned.1.call-done = bf16[1024,768]{1,0:T(8,128)(2,1)} async-done(((bf16[256,768]{1,0:T(8,128)(2,1)}), bf16[1024,768]{1,0:T(8,128)(2,1)}) %all-gather.8.cloned.1.call-update) | async-done | bytes 1572880 | tf_op jit(solution)/shard_map/all_gather | solution.py:76
  332.1 94.6 %while.110 = (s32[]{:T(128)}, f32[4,256]{1,0:T(4,128)S(1)}, f32[4,256]{1,0:T(4,128)S(1)}, f32[4,256]{1,0:T(4,128)S(1)}, bf16[4,256,768]{2,1,0:T(8,128)(2,1)}, /*...) while((s32[]{:T(128)}, f32[4,256]{1,0:T(4,128)S(1)}, ...), condition=%wide.region_28.30_spmd, body=%wide.region_25.29_spmd.sunk | while | flops 3164483584 | bytes 29207416 | solution.py:364
  332.1 11.3 %fusion.519 = (f32[256]{0:T(256)S(1)}, f32[256,8032]{0,1:T(8,128)}) fusion(bf16[8032,768]{1,0:T(8,128)(2,1)} %get-tuple-element.1780, bf16[4,256,768]{2,1,0:T(8,128)(2,1)} %get-tuple-element.1779, s32[]{:T(128)} %get-tuple-element.1765), kind=kOutput, calls=%fused_computation.567.clone.1 | convolution fusion | flops 3160366848 | bytes 20956672 | tf_op jit(solution)/shard_map/while/body/eval_jaxpr/dot_general | solution.py:356
  343.4 7.2 gather_fusion
  350.7 4.5 exponential_reduce_fusion.2
  355.3 11.3 %fusion.519 = (f32[256]{0:T(256)S(1)}, f32[256,8032]{0,1:T(8,128)}) fusion(bf16[8032,768]{1,0:T(8,128)(2,1)} %get-tuple-element.1780, bf16[4,256,768]{2,1,0:T(8,128)(2,1)} %get-tuple-element.1779, s32[]{:T(128)} %get-tuple-element.1765), kind=kOutput, calls=%fused_computation.567.clone.1 | convolution fusion | flops 3160366848 | bytes 20956672 | tf_op jit(solution)/shard_map/while/body/eval_jaxpr/dot_general | solution.py:356
  366.7 7.8 gather_fusion
  374.6 4.5 exponential_reduce_fusion.2
  379.1 11.3 %fusion.519 = (f32[256]{0:T(256)S(1)}, f32[256,8032]{0,1:T(8,128)}) fusion(bf16[8032,768]{1,0:T(8,128)(2,1)} %get-tuple-element.1780, bf16[4,256,768]{2,1,0:T(8,128)(2,1)} %get-tuple-element.1779, s32[]{:T(128)} %get-tuple-element.1765), kind=kOutput, calls=%fused_computation.567.clone.1 | convolution fusion | flops 3160366848 | bytes 20956672 | tf_op jit(solution)/shard_map/while/body/eval_jaxpr/dot_general | solution.py:356
  390.5 7.8 gather_fusion
  398.4 4.5 exponential_reduce_fusion.2
  403.0 11.3 %fusion.519 = (f32[256]{0:T(256)S(1)}, f32[256,8032]{0,1:T(8,128)}) fusion(bf16[8032,768]{1,0:T(8,128)(2,1)} %get-tuple-element.1780, bf16[4,256,768]{2,1,0:T(8,128)(2,1)} %get-tuple-element.1779, s32[]{:T(128)} %get-tuple-element.1765), kind=kOutput, calls=%fused_computation.567.clone.1 | convolution fusion | flops 3160366848 | bytes 20956672 | tf_op jit(solution)/shard_map/while/body/eval_jaxpr/dot_general | solution.py:356
  414.4 7.7 gather_fusion
  422.1 4.5 exponential_reduce_fusion.2
  444.0 3.1 collective-permute-start.10
  448.3 86.3 %while.111 = (s32[]{:T(128)}, f32[4,256,768]{2,1,0:T(8,128)}, f32[4,256]{1,0:T(4,128)S(1)}, bf16[4,256,768]{2,1,0:T(8,128)(2,1)}, bf16[8032,768]{1,0:T(8,128)(2,...) while((s32[]{:T(128)}, f32[4,256,768]{2,1,0:T(8,128)}, ...), condition=%wide.region_34.36_spmd, body=%wide.region_33.35_spmd.sunk | while | flops 6331015168 | bytes 25865064 | solution.py:400
  448.3 21.4 %fusion.524 = f32[4,256,768]{2,1,0:T(8,128)} fusion(f32[4,256,768]{2,1,0:T(8,128)} %get-tuple-element.1795, s32[]{:T(128)} %get-tuple-element.1794, bf16[8032,768]{1,0:T(8,128)(2,1)} %get-tuple-element.1807, s32[256]{0:T(256)S(1)} %bitcast.810, f32[256]{0:T(256)S(1)} %bitcast.811, f32[256]{0:T(256)S(1)} %bitcast.812, ...), kind=kOutput, calls=%fused_computation.175.clone.1 | convolution fusion | flops 6331015168 | bytes 25858304 | tf_op jit(solution)/shard_map/while/body/eval_jaxpr/dot_general | solution.py:391
  469.8 21.4 %fusion.524 = f32[4,256,768]{2,1,0:T(8,128)} fusion(f32[4,256,768]{2,1,0:T(8,128)} %get-tuple-element.1795, s32[]{:T(128)} %get-tuple-element.1794, bf16[8032,768]{1,0:T(8,128)(2,1)} %get-tuple-element.1807, s32[256]{0:T(256)S(1)} %bitcast.810, f32[256]{0:T(256)S(1)} %bitcast.811, f32[256]{0:T(256)S(1)} %bitcast.812, ...), kind=kOutput, calls=%fused_computation.175.clone.1 | convolution fusion | flops 6331015168 | bytes 25858304 | tf_op jit(solution)/shard_map/while/body/eval_jaxpr/dot_general | solution.py:391
  491.2 21.5 %fusion.524 = f32[4,256,768]{2,1,0:T(8,128)} fusion(f32[4,256,768]{2,1,0:T(8,128)} %get-tuple-element.1795, s32[]{:T(128)} %get-tuple-element.1794, bf16[8032,768]{1,0:T(8,128)(2,1)} %get-tuple-element.1807, s32[256]{0:T(256)S(1)} %bitcast.810, f32[256]{0:T(256)S(1)} %bitcast.811, f32[256]{0:T(256)S(1)} %bitcast.812, ...), kind=kOutput, calls=%fused_computation.175.clone.1 | convolution fusion | flops 6331015168 | bytes 25858304 | tf_op jit(solution)/shard_map/while/body/eval_jaxpr/dot_general | solution.py:391
  512.7 21.4 %fusion.524 = f32[4,256,768]{2,1,0:T(8,128)} fusion(f32[4,256,768]{2,1,0:T(8,128)} %get-tuple-element.1795, s32[]{:T(128)} %get-tuple-element.1794, bf16[8032,768]{1,0:T(8,128)(2,1)} %get-tuple-element.1807, s32[256]{0:T(256)S(1)} %bitcast.810, f32[256]{0:T(256)S(1)} %bitcast.811, f32[256]{0:T(256)S(1)} %bitcast.812, ...), kind=kOutput, calls=%fused_computation.175.clone.1 | convolution fusion | flops 6331015168 | bytes 25858304 | tf_op jit(solution)/shard_map/while/body/eval_jaxpr/dot_general | solution.py:391
  537.2 57.8 %reduce-scatter.8.cloned.1.call-done = f32[256,768]{1,0:T(8,128)} async-done(((f32[1024,768]{1,0:T(8,128)}), f32[256,768]{1,0:T(8,128)}) %reduce-scatter.8.cloned.1.call-update) | async-done | bytes 786448 | tf_op jit(solution)/shard_map/reduce_scatter | solution.py:80
  597.2 8.9 %multiply_reduce_fusion.6 = (f32[256]{0:T(256)S(1)}, f32[256,768]{1,0:T(8,128)}) fusion(f32[256,768]{1,0:T(8,128)} %get-tuple-element.1103, f32[768]{0:T(1024)S(1)} %copy-done.106, bf16[3072,1536]{1,0:T(8,128)(2,1)} %all-gather.6.cloned.1.call-done, f32[256,3072]{1,0:T(8,128)} %copy-done.123, f32[256,768]{1,0:T(8,128)} %copy-done.25, ...), kind=kOutput, calls=%fused_computation.352 | convolution fusion | flops 2420047616 | bytes 15737856 | tf_op jit(solution)/shard_map/dot_general | solution.py:181
  613.7 4.1 all-to-all-start.6
  621.3 4.1 collective-permute-done.18
  632.6 30.9 %while.112 = (s32[]{:T(128)}, f32[1024,3,64]{0,2,1:T(8,128)S(1)}, f32[1024,3,64]{0,2,1:T(8,128)}, bf16[2,512,3,64]{1,3,2,0:T(8,128)(2,1)}, bf16[2,512,3,64]{1,3,...) while((s32[]{:T(128)}, f32[1024,3,64]{0,2,1:T(8,128)S(1)}, ...), condition=%wide.region_40.42_spmd.clone, body=%wide.region_38.41_spmd.clone.sunk | while | flops 1023965696 | bytes 123006320 | solution.py:176
  633.0 3.1 exponential_divide_fusion.6
  647.9 3.1 exponential_divide_fusion.6
  671.0 4.4 all-to-all-start.7
  676.7 14.6 %all-to-all-done.7 = bf16[4,3,256,192]{2,3,1,0:T(8,128)(2,1)} async-done(((bf16[4,3,256,192]{2,3,1,0:T(8,128)(2,1)}), bf16[4,3,256,192]{2,3,1,0:T(8,128)(2,1)}, u32[]{:S(2)}, u32[]{:S(2)}) %all-to-all-start.7) | async-done | bytes 1179680 | tf_op jit(solution)/shard_map/all_to_all | solution.py:84
  701.7 4.4 all-to-all-start.9
  712.2 8.7 %multiply_reduce_fusion.4 = (f32[256]{0:T(256)S(1)}, f32[256,768]{1,0:T(8,128)}) fusion(f32[256,768]{1,0:T(8,128)} %copy-done.39, f32[768]{0:T(1024)S(1)} %copy-done.105, bf16[3072,1536]{1,0:T(8,128)(2,1)} %all-gather.4.cloned.1.call-done, f32[256,3072]{1,0:T(8,128)} %copy-done.122, f32[256,768]{1,0:T(8,128)S(1)} %copy-done.24, ...), kind=kOutput, calls=%fused_computation.350 | convolution fusion | flops 2419851008 | bytes 15734784 | tf_op jit(solution)/shard_map/dot_general | solution.py:181
  721.0 3.7 convolution_convert_fusion.1
  728.3 4.1 all-to-all-start.8
  736.5 27.5 %while.114 = (s32[]{:T(128)}, f32[1024,3,64]{0,2,1:T(8,128)S(1)}, bf16[2,512,3,64]{1,3,2,0:T(8,128)(2,1)}, bf16[2,512,3,64]{1,3,2,0:T(8,128)(2,1)S(1)}, s32[2,51...) while((s32[]{:T(128)}, f32[1024,3,64]{0,2,1:T(8,128)S(1)}, ...), condition=%wide.region_49.51_spmd.clone, body=%wide.region_47.50_spmd.clone.sunk | while | flops 823098368 | bytes 67763400 | solution.py:176
  746.7 3.5 fusion.552
  760.5 3.5 fusion.552
  770.7 23.2 %while.113 = (s32[]{:T(128)}, f32[1024,3,64]{0,2,1:T(8,128)S(1)}, bf16[2,512,3,64]{1,3,2,0:T(8,128)(2,1)}, bf16[2,512,3,64]{1,3,2,0:T(8,128)(2,1)S(1)}, s32[2,51...) while((s32[]{:T(128)}, f32[1024,3,64]{0,2,1:T(8,128)S(1)}, ...), condition=%wide.region_45.47_spmd.clone, body=%wide.region_43.46_spmd.clone.sunk | while | flops 822049280 | bytes 67759280 | solution.py:176
  778.7 3.5 fusion.543
  782.7 3.1 exponential_divide_fusion.7
  790.3 3.5 fusion.543
  814.7 3.5 collective-permute-done.29
  824.8 3.7 collective-permute-done.31
  841.1 4.5 collective-permute-start.7
  846.8 11.3 %collective-permute-done.27 = f32[8,8,768]{2,1,0:T(8,128)S(1)} collective-permute-done((f32[8,8,768]{2,1,0:T(8,128)S(1)}, f32[8,8,768]{2,1,0:T(8,128)S(1)}, u32[]{:S(2)}, u32[]{:S(2)}) %collective-permute-start.27) | collective-permute-done | bytes 196640 | tf_op jit(solution)/shard_map/ppermute | solution.py:25
  (748 shorter events, 321.7 us)
Async XLA Ops:
  8.0 823.3 %copy-start = (bf16[6,14,8,768]{3,2,1,0:T(8,128)(2,1)S(1)}, bf16[6,14,8,768]{3,2,1,0:T(8,128)(2,1)}, u32[]{:S(2)}) copy-start(bf16[6,14,8,768]{3,2,1,0:T(8,128)(2,1)} %param.48) | copy-start | bytes 3096580
  8.0 60.4 %reduce-scatter.4.cloned.1.call-start = ((), (), s32[]{:S(2)}) async-start(), calls=%async_computation.13 | async-start | bytes 1966080 | tf_op jit(solution)/shard_map/reduce_scatter | solution.py:80
  8.9 5.6 collective-permute-start
  11.9 4.5 collective-permute-start.1
  14.5 5.4 collective-permute-start.2
  33.9 81.6 %reduce-scatter.6.cloned.1.call-start = ((), (), s32[]{:S(2)}) async-start(), calls=%async_computation.14 | async-start | bytes 1966080 | tf_op jit(solution)/shard_map/reduce_scatter | solution.py:80
  46.3 161.6 %all-gather.4.cloned.1.call-start = ((), (), s32[]{:S(2)}) async-start(), calls=%async_computation.15 | async-start | bytes 9732096 | tf_op jit(solution)/shard_map/all_gather | solution.py:334
  50.0 233.4 %all-gather.6.cloned.1.call-start = ((), (), s32[]{:S(2)}) async-start(), calls=%async_computation.16 | async-start | bytes 9732096 | tf_op jit(solution)/shard_map/all_gather | solution.py:334
  52.1 165.7 %copy-start.60 = (bf16[6,8,768]{2,1,0:T(8,128)(2,1)}, bf16[6,8,768]{2,1,0:T(8,128)(2,1)S(1)}, u32[]{:S(2)}) copy-start(bf16[6,8,768]{2,1,0:T(8,128)(2,1)S(1)} %convert_element_type.240) | copy-start | bytes 221188
  52.1 167.7 %copy-start.40 = (bf16[6,8,768]{2,1,0:T(8,128)(2,1)}, bf16[6,8,768]{2,1,0:T(8,128)(2,1)S(1)}, u32[]{:S(2)}) copy-start(bf16[6,8,768]{2,1,0:T(8,128)(2,1)S(1)} %convert_element_type.242) | copy-start | bytes 221188
  78.8 37.9 %copy-start.103 = (f32[768]{0:T(1024)S(1)}, f32[768]{0:T(1024)}, u32[]{:S(2)}) copy-start(f32[768]{0:T(1024)} %get-tuple-element.822) | copy-start | bytes 9220
  80.2 49.8 %all-to-all-start = ((bf16[4,3,256,192]{2,3,1,0:T(8,128)(2,1)}), bf16[4,3,256,192]{2,3,1,0:T(8,128)(2,1)S(1)}, u32[]{:S(2)}, u32[]{:S(2)}) async-start(bf16[4,3,256,192]{2,3,1,0:T(8,128)(2,1)} %copy.193), calls=%async_computation.1 | async-start | bytes 2359296 | tf_op jit(solution)/shard_map/all_to_all | solution.py:84
  130.0 36.5 %all-to-all-start.2 = ((bf16[4,3,256,192]{2,3,1,0:T(8,128)(2,1)}), bf16[4,3,256,192]{2,3,1,0:T(8,128)(2,1)S(1)}, u32[]{:S(2)}, u32[]{:S(2)}) async-start(bf16[4,3,256,192]{2,3,1,0:T(8,128)(2,1)} %copy.204), calls=%async_computation.4 | async-start | bytes 2359296 | tf_op jit(solution)/shard_map/all_to_all | solution.py:84
  166.5 23.4 %all-to-all-start.1 = ((bf16[4,256,192]{1,2,0:T(8,128)(2,1)}), bf16[4,256,192]{1,2,0:T(8,128)(2,1)}, u32[]{:S(2)}, u32[]{:S(2)}) async-start(bf16[4,256,192]{1,2,0:T(8,128)(2,1)} %copy.199), calls=%async_computation.2 | async-start | bytes 786432 | tf_op jit(solution)/shard_map/all_to_all | solution.py:84
  189.9 15.4 %all-to-all-start.3 = ((bf16[4,256,192]{1,2,0:T(8,128)(2,1)}), bf16[4,256,192]{1,2,0:T(8,128)(2,1)}, u32[]{:S(2)}, u32[]{:S(2)}) async-start(bf16[4,256,192]{1,2,0:T(8,128)(2,1)} %copy.210), calls=%async_computation.5 | async-start | bytes 786432 | tf_op jit(solution)/shard_map/all_to_all | solution.py:84
  196.0 84.7 %copy-start.20 = (f32[256,768]{1,0:T(8,128)}, f32[256,768]{1,0:T(8,128)S(1)}, u32[]{:S(2)}) copy-start(f32[256,768]{1,0:T(8,128)S(1)} %get-tuple-element.1101) | copy-start | bytes 2359300
  227.0 21.3 %all-to-all-start.4 = ((bf16[4,3,256,192]{2,3,1,0:T(8,128)(2,1)}), bf16[4,3,256,192]{2,3,1,0:T(8,128)(2,1)S(1)}, u32[]{:S(2)}, u32[]{:S(2)}) async-start(bf16[4,3,256,192]{2,3,1,0:T(8,128)(2,1)} %copy.213), calls=%async_computation.6 | async-start | bytes 2359296 | tf_op jit(solution)/shard_map/all_to_all | solution.py:84
  230.5 101.5 %all-gather.8.cloned.1.call-start = ((), (), s32[]{:S(2)}) async-start(), calls=%async_computation.17 | async-start | bytes 1966080 | tf_op jit(solution)/shard_map/all_gather | solution.py:76
  294.9 300.2 %reduce-scatter.8.cloned.1.call-start = ((), (), s32[]{:S(2)}) async-start(), calls=%async_computation.18 | async-start | bytes 3932160 | tf_op jit(solution)/shard_map/reduce_scatter | solution.py:80
  332.1 104.5 %copy-start.59 = (s32[4,4,4,64]{3,2,1,0:T(4,128)S(1)}, s32[4,4,4,64]{3,2,1,0:T(4,128)}, u32[]{:S(2)}) copy-start(s32[4,4,4,64]{3,2,1,0:T(4,128)} %copy-done.58) | copy-start | bytes 49156
  426.8 4.7 collective-permute-start.3
  431.5 4.7 collective-permute-start.4
  437.2 3.7 collective-permute-start.8
  442.1 1.2 collective-permute-start.9
  444.0 3.6 collective-permute-start.10
  448.3 86.4 %copy-start.41 = (bf16[6,8,768]{2,1,0:T(8,128)(2,1)S(1)}, bf16[6,8,768]{2,1,0:T(8,128)(2,1)}, u32[]{:S(2)}) copy-start(bf16[6,8,768]{2,1,0:T(8,128)(2,1)} %copy-done.40) | copy-start | bytes 221188
  448.3 87.0 %copy-start.91 = (bf16[256,8]{0,1:T(8,128)(2,1)S(1)}, bf16[256,8]{0,1:T(8,128)(2,1)}, u32[]{:S(2)}) copy-start(bf16[256,8]{0,1:T(8,128)(2,1)} %copy-done.90) | copy-start | bytes 12292
  448.3 87.0 %copy-start.93 = (bf16[256,8]{0,1:T(8,128)(2,1)S(1)}, bf16[256,8]{0,1:T(8,128)(2,1)}, u32[]{:S(2)}) copy-start(bf16[256,8]{0,1:T(8,128)(2,1)} %copy-done.92) | copy-start | bytes 12292
  535.3 84.7 %collective-permute-start.20 = (bf16[16,256]{1,0:T(8,128)(2,1)S(1)}, bf16[16,256]{1,0:T(8,128)(2,1)S(1)}, u32[]{:S(2)}, u32[]{:S(2)}) collective-permute-start(bf16[16,256]{1,0:T(8,128)(2,1)S(1)} %get-tuple-element.1093), channel_id=1, source_target_pairs={{0,4},{4,0},{8,12},{12,8},{1,5},{5,1},{9,13},{13,9},{2,6},{6,2},{1... | collective-permute-start | bytes 24584 | tf_op jit(solution)/shard_map/ppermute | solution.py:25
  535.4 84.7 %collective-permute-start.21 = (bf16[16,256]{1,0:T(8,128)(2,1)S(1)}, bf16[16,256]{1,0:T(8,128)(2,1)}, u32[]{:S(2)}, u32[]{:S(2)}) collective-permute-start(bf16[16,256]{1,0:T(8,128)(2,1)S(1)} %get-tuple-element.1093), channel_id=1, source_target_pairs={{0,8},{4,12},{8,0},{12,4},{1,9},{5,13},{9,1},{13,5},{2,10},{6,14},... | collective-permute-start | bytes 24584 | tf_op jit(solution)/shard_map/ppermute | solution.py:25
  537.2 82.8 %collective-permute-start.22 = (bf16[16,256]{1,0:T(8,128)(2,1)S(1)}, bf16[16,256]{1,0:T(8,128)(2,1)}, u32[]{:S(2)}, u32[]{:S(2)}) collective-permute-start(bf16[16,256]{1,0:T(8,128)(2,1)S(1)} %get-tuple-element.1093), channel_id=1, source_target_pairs={{0,12},{4,8},{8,4},{12,0},{1,13},{5,9},{9,5},{13,1},{2,14},{6,10},... | collective-permute-start | bytes 24584 | tf_op jit(solution)/shard_map/ppermute | solution.py:25
  613.7 12.4 %all-to-all-start.6 = ((bf16[4,256,192]{1,2,0:T(8,128)(2,1)}), bf16[4,256,192]{1,2,0:T(8,128)(2,1)}, u32[]{:S(2)}, u32[]{:S(2)}) async-start(bf16[4,256,192]{1,2,0:T(8,128)(2,1)} %bitcast.775), calls=%async_computation.9 | async-start | bytes 786432 | tf_op jit(solution)/shard_map/all_to_all | solution.py:84
  617.8 3.5 collective-permute-start.17
  618.3 7.1 collective-permute-start.18
  620.0 5.5 collective-permute-start.19
  671.0 20.3 %all-to-all-start.7 = ((bf16[4,3,256,192]{2,3,1,0:T(8,128)(2,1)}), bf16[4,3,256,192]{2,3,1,0:T(8,128)(2,1)}, u32[]{:S(2)}, u32[]{:S(2)}) async-start(bf16[4,3,256,192]{2,3,1,0:T(8,128)(2,1)} %copy.225), calls=%async_computation.10 | async-start | bytes 2359296 | tf_op jit(solution)/shard_map/all_to_all | solution.py:84
  695.6 31.5 %copy-start.46 = (f32[1,8,768]{2,1,0:T(8,128)}, f32[1,8,768]{2,1,0:T(8,128)S(1)}, u32[]{:S(2)}) copy-start(f32[1,8,768]{2,1,0:T(8,128)S(1)} %convolution_bitcast_fusion.2) | copy-start | bytes 73732
  701.7 26.6 %all-to-all-start.9 = ((bf16[4,256,192]{1,2,0:T(8,128)(2,1)}), bf16[4,256,192]{1,2,0:T(8,128)(2,1)}, u32[]{:S(2)}, u32[]{:S(2)}) async-start(bf16[4,256,192]{1,2,0:T(8,128)(2,1)} %bitcast.774), calls=%async_computation.12 | async-start | bytes 786432 | tf_op jit(solution)/shard_map/all_to_all | solution.py:84
  727.8 83.7 %collective-permute-start.28 = (f32[4,8,768]{2,1,0:T(8,128)}, f32[4,8,768]{2,1,0:T(8,128)}, u32[]{:S(2)}, u32[]{:S(2)}) collective-permute-start(f32[4,8,768]{2,1,0:T(8,128)} %pad_maximum_fusion.6), channel_id=1, source_target_pairs={{0,4},{4,0},{8,12},{12,8},{1,5},{5,1},{9,13},{13,9},{2,6},{6,2},{1... | collective-permute-start | bytes 294920 | tf_op jit(solution)/shard_map/ppermute | solution.py:25
  728.3 38.1 %all-to-all-start.8 = ((bf16[4,256,192]{1,2,0:T(8,128)(2,1)}), bf16[4,256,192]{1,2,0:T(8,128)(2,1)}, u32[]{:S(2)}, u32[]{:S(2)}) async-start(bf16[4,256,192]{1,2,0:T(8,128)(2,1)} %bitcast.124), calls=%async_computation.11 | async-start | bytes 786432 | tf_op jit(solution)/shard_map/all_to_all | solution.py:84
  799.1 32.1 %copy-start.38 = (f32[6,8,768]{2,1,0:T(8,128)S(1)}, f32[6,8,768]{2,1,0:T(8,128)}, u32[]{:S(2)}) copy-start(f32[6,8,768]{2,1,0:T(8,128)} %param.49) | copy-start | bytes 442372
  801.6 4.2 collective-permute-start.11
  802.1 5.3 collective-permute-start.12
  803.7 3.7 collective-permute-start.13
  803.9 6.2 collective-permute-start.14
  805.8 4.3 collective-permute-start.15
  807.4 3.2 collective-permute-start.16
  808.8 49.4 %copy-start.45 = (f32[6,8,768]{2,1,0:T(8,128)S(1)}, f32[6,8,768]{2,1,0:T(8,128)}, u32[]{:S(2)}) copy-start(f32[6,8,768]{2,1,0:T(8,128)} %param.50) | copy-start | bytes 442372
  808.8 49.4 %copy-start.65 = (f32[6,8,768]{2,1,0:T(8,128)S(1)}, f32[6,8,768]{2,1,0:T(8,128)}, u32[]{:S(2)}) copy-start(f32[6,8,768]{2,1,0:T(8,128)} %param.54) | copy-start | bytes 442372
  808.8 49.4 %copy-start.66 = (f32[6,8,768]{2,1,0:T(8,128)S(1)}, f32[6,8,768]{2,1,0:T(8,128)}, u32[]{:S(2)}) copy-start(f32[6,8,768]{2,1,0:T(8,128)} %param.53) | copy-start | bytes 442372
  810.7 49.5 %copy-start.67 = (f32[6,8,768]{2,1,0:T(8,128)S(1)}, f32[6,8,768]{2,1,0:T(8,128)}, u32[]{:S(2)}) copy-start(f32[6,8,768]{2,1,0:T(8,128)} %param.52) | copy-start | bytes 442372
  810.7 49.5 %copy-start.68 = (f32[6,8,768]{2,1,0:T(8,128)S(1)}, f32[6,8,768]{2,1,0:T(8,128)}, u32[]{:S(2)}) copy-start(f32[6,8,768]{2,1,0:T(8,128)} %param.51) | copy-start | bytes 442372
  811.3 2.7 collective-permute-start.23
  812.5 5.7 collective-permute-start.29
  814.0 7.8 collective-permute-start.24
  819.1 4.7 collective-permute-start.30
  821.9 9.0 %collective-permute-start.25 = (f32[8,8,768]{2,1,0:T(8,128)S(1)}, f32[8,8,768]{2,1,0:T(8,128)S(1)}, u32[]{:S(2)}, u32[]{:S(2)}) collective-permute-start(f32[8,8,768]{2,1,0:T(8,128)S(1)} %add.510), channel_id=1, source_target_pairs={{0,16},{16,0},{1,17},{17,1},{2,18},{18,2},{3,19},{19,3},{4,20},{20... | collective-permute-start | bytes 589832 | tf_op jit(solution)/shard_map/ppermute | solution.py:25
  823.8 4.7 collective-permute-start.31
  828.5 18.0 %collective-permute-start.32 = (f32[4,8,768]{2,1,0:T(8,128)S(1)}, f32[4,8,768]{2,1,0:T(8,128)S(1)}, u32[]{:S(2)}, u32[]{:S(2)}) collective-permute-start(f32[4,8,768]{2,1,0:T(8,128)S(1)} %add.517), channel_id=1, source_target_pairs={{0,2},{1,3},{2,0},{3,1},{4,6},{5,7},{6,4},{7,5},{8,10},{9,11},{10,... | collective-permute-start | bytes 294920 | tf_op jit(solution)/shard_map/ppermute | solution.py:25
  830.9 15.6 %collective-permute-start.26 = (f32[8,8,768]{2,1,0:T(8,128)S(1)}, f32[8,8,768]{2,1,0:T(8,128)S(1)}, u32[]{:S(2)}, u32[]{:S(2)}) collective-permute-start(f32[8,8,768]{2,1,0:T(8,128)S(1)} %add.511), channel_id=1, source_target_pairs={{0,1},{1,0},{2,3},{3,2},{4,5},{5,4},{6,7},{7,6},{8,9},{9,8},{10,11... | collective-permute-start | bytes 589832 | tf_op jit(solution)/shard_map/ppermute | solution.py:25
  834.2 3.6 collective-permute-start.5
  839.2 1.2 collective-permute-start.6
  841.1 4.7 collective-permute-start.7
  846.6 11.5 %collective-permute-start.27 = (f32[8,8,768]{2,1,0:T(8,128)S(1)}, f32[8,8,768]{2,1,0:T(8,128)S(1)}, u32[]{:S(2)}, u32[]{:S(2)}) collective-permute-start(f32[8,8,768]{2,1,0:T(8,128)S(1)} %add.512), channel_id=1, source_target_pairs={{0,2},{1,3},{2,0},{3,1},{4,6},{5,7},{6,4},{7,5},{8,10},{9,11},{10,... | collective-permute-start | bytes 589832 | tf_op jit(solution)/shard_map/ppermute | solution.py:25
  (118 other events, 1021.6 us)
Sparse Core Ops, SparseCore 0:
  34.0 34.3 reduce-scatter.3
  70.7 44.6 reduce-scatter.5
  295.0 37.0 all-gather.7
  534.7 60.3 reduce-scatter.7
Sparse Core Ops, SparseCore 1:
  50.1 109.7 all-gather.3
  162.5 87.7 all-gather.5

commit v2 on v1

--- a/solution.py
+++ b/solution.py
@@ -1,6 +1,10 @@
+import functools
+
 import jax
 import jax.numpy as jnp
 from jax import lax
+from jax.experimental import pallas as pl
+from jax.experimental.pallas import tpu as pltpu
 from jax.sharding import PartitionSpec as P
 
 MODEL_DIMENSION = 768
@@ -348,56 +352,121 @@
     return contract(grad_pre, units[:, :model_width], 1, 0)
 
 
-def vocab_stats(head_rows, clipped, inside, embedding, n_col):
-    model_width = head_rows.shape[1]
-
-    def one_block(members):
-        rows_blk, clip_blk, inside_blk = members
-        logits = lax.dot_general(
-            rows_blk, embedding, (((1,), (1,)), ((), ())), preferred_element_type=jnp.float32
-        )
-        row_top = jnp.max(logits, axis=1)
-        row_total = jnp.sum(jnp.exp(logits - row_top[:, None]), axis=1)
-        picked = jnp.take_along_axis(logits, clip_blk[:, None], axis=1)[:, 0]
-        return (row_top, row_total, jnp.where(inside_blk, picked, 0.0))
-
-    block_outs = lax.map(
-        one_block,
-        (
-            head_rows.reshape(n_col, -1, model_width),
-            clipped.reshape(n_col, -1),
-            inside.reshape(n_col, -1),
-        ),
-    )
-    return tuple((member.reshape(-1) for member in block_outs))
-
-
-def vocab_back(head_rows, clipped, inside, embedding, n_col, log_total, coef_rows):
-    model_width = head_rows.shape[1]
-    vocab_part = embedding.shape[0]
-
-    def one_block(members):
-        rows_blk, clip_blk, inside_blk, total_blk, coef_blk = members
-        logits = lax.dot_general(
-            rows_blk, embedding, (((1,), (1,)), ((), ())), preferred_element_type=jnp.float32
-        )
-        probs_f = jnp.exp(logits - total_blk[:, None])
-        hits = (jnp.arange(vocab_part, dtype=jnp.int32)[None, :] == clip_blk[:, None]) & inside_blk[
-            :, None
-        ]
-        grad_logits = (coef_blk[:, None] * (probs_f - hits.astype(jnp.float32))).astype(
-            jnp.bfloat16
-        )
-        return jnp.dot(grad_logits, embedding, preferred_element_type=jnp.float32)
-
-    members = (
-        head_rows.reshape(n_col, -1, model_width),
-        clipped.reshape(n_col, -1),
-        inside.reshape(n_col, -1),
-        log_total.reshape(n_col, -1),
-        coef_rows.reshape(n_col, -1),
-    )
-    return lax.map(one_block, members).reshape(-1, model_width)
+def head_kernel(chunk, block, rows_ref, target_ref, table_ref, acc_ref, total_ref, base_ref, held, top_ref, sems):
+    vocab_part = table_ref.shape[0]
+    full = vocab_part // chunk
+    tail = vocab_part - full * chunk
+    tail_wide = -(-tail // 128) * 128
+    blocks = rows_ref.shape[0] // block
+    copies = [
+        pltpu.make_async_copy(
+            table_ref.at[pl.ds(at * chunk, size)], held.at[pl.ds(at * chunk, size)], sems.at[at]
+        )
+        for at, size in enumerate([chunk] * full + [tail] * (tail > 0))
+    ]
+    for copy in copies:
+        copy.start()
+    if tail_wide > tail:
+        held[pl.ds(vocab_part, tail_wide - tail), :] = jnp.zeros(
+            (tail_wide - tail, held.shape[1]), held.dtype
+        )
+
+    def dots(at, offset, width):
+        return lax.dot_general(
+            rows_ref[pl.ds(at * block, block), :],
+            held[pl.ds(offset, width), :],
+            (((1,), (1,)), ((), ())),
+            preferred_element_type=jnp.float32,
+        )
+
+    def one_chunk(offset, width, used):
+        table = held[pl.ds(offset, width), :]
+        for at in range(blocks):
+            rows_at = pl.ds(at * block, block)
+            logits = dots(at, offset, width)
+            places = lax.broadcasted_iota(jnp.int32, logits.shape, 1)
+            if used < width:
+                logits = jnp.where(places < used, logits, -1e30)
+            weights = jnp.exp(logits - base_ref[rows_at, :])
+            top_ref[rows_at, :] = jnp.maximum(
+                top_ref[rows_at, :], jnp.max(logits, axis=1, keepdims=True)
+            )
+            total_ref[rows_at, :] += jnp.sum(weights, axis=1, keepdims=True)
+            hit = places == target_ref[rows_at, :] - offset
+            kept = jnp.where(hit, 0.0, weights).astype(jnp.bfloat16)
+            acc_ref[rows_at, :] += jnp.dot(kept, table, preferred_element_type=jnp.float32)
+
+    def one_pass(wait):
+        acc_ref[...] = jnp.zeros_like(acc_ref)
+        total_ref[...] = jnp.zeros_like(total_ref)
+
+        def body(at, carry):
+            if wait:
+                pltpu.make_async_copy(
+                    table_ref.at[pl.ds(0, chunk)], held.at[pl.ds(0, chunk)], sems.at[at]
+                ).wait()
+            one_chunk(pl.multiple_of(at * chunk, chunk), chunk, chunk)
+            return carry
+
+        lax.fori_loop(0, full, body, 0)
+        if tail:
+            if wait:
+                copies[full].wait()
+            one_chunk(full * chunk, tail_wide, tail)
+
+    copies[0].wait()
+    sample = min(256, chunk)
+    for at in range(blocks):
+        base_ref[pl.ds(at * block, block), :] = jnp.max(
+            dots(at, 0, sample), axis=1, keepdims=True
+        )
+    top_ref[...] = base_ref[...]
+
+    acc_ref[...] = jnp.zeros_like(acc_ref)
+    total_ref[...] = jnp.zeros_like(total_ref)
+    one_chunk(0, chunk, chunk)
+
+    def body(at, carry):
+        pltpu.make_async_copy(
+            table_ref.at[pl.ds(0, chunk)], held.at[pl.ds(0, chunk)], sems.at[at]
+        ).wait()
+        one_chunk(pl.multiple_of(at * chunk, chunk), chunk, chunk)
+        return carry
+
+    lax.fori_loop(1, full, body, 0)
+    if tail:
+        copies[full].wait()
+        one_chunk(full * chunk, tail_wide, tail)
+
+    @pl.when(jnp.max(top_ref[...] - base_ref[...]) > 40.0)
+    def _():
+        base_ref[...] = top_ref[...]
+        one_pass(False)
+
+
+def head_pass(rows, targets, table, chunk=1024, block=256):
+    tokens, width = rows.shape
+    vocab_part = table.shape[0]
+    full = vocab_part // chunk
+    tail = vocab_part - full * chunk
+    held_rows = full * chunk + -(-tail // 128) * 128
+    column = jax.ShapeDtypeStruct((tokens, 1), jnp.float32)
+    return pl.pallas_call(
+        functools.partial(head_kernel, chunk, block),
+        out_shape=(jax.ShapeDtypeStruct((tokens, width), jnp.float32), column, column),
+        in_specs=[
+            pl.BlockSpec(memory_space=pltpu.VMEM),
+            pl.BlockSpec(memory_space=pltpu.VMEM),
+            pl.BlockSpec(memory_space=pl.ANY),
+        ],
+        out_specs=tuple([pl.BlockSpec(memory_space=pltpu.VMEM)] * 3),
+        scratch_shapes=[
+            pltpu.VMEM((held_rows, width), table.dtype),
+            pltpu.VMEM((tokens, 1), jnp.float32),
+            pltpu.SemaphoreType.DMA((full + (tail > 0),)),
+        ],
+        compiler_params=pltpu.CompilerParams(vmem_limit_bytes=56 * 1024 * 1024),
+    )(rows, targets, table)
 
 
 def merge_stats(left_side, right_side):
@@ -509,8 +578,15 @@
     head_rows = col_rows(final_rows)
     local_t = target_all - col_at * vocab_part
     inside = (local_t >= 0) & (local_t < vocab_part)
-    clipped = jnp.clip(local_t, 0, vocab_part - 1)
-    stats = vocab_stats(head_rows, clipped, inside, embedding, n_col)
+    target_rows = jnp.take(
+        embedding, jnp.clip(local_t, 0, vocab_part - 1), axis=0
+    ).astype(jnp.float32)
+    grad_rows, total_part, base_part = head_pass(head_rows, local_t[:, None], embedding)
+    target_part = jnp.where(
+        inside, jnp.sum(head_rows.astype(jnp.float32) * target_rows, axis=1), 0.0
+    )
+    base_part = base_part[:, 0]
+    stats = (base_part, total_part[:, 0], target_part)
     step = 1
     while step < n_col:
         others = swapped(jnp.stack(stats), "col", step)
@@ -518,12 +594,15 @@
         step *= 2
     row_top, row_total, row_target = stats
     log_total = row_top + jnp.log(row_total)
-    ce_local = jnp.sum(mask_float * (log_total - row_target))
-    ce_total = summed(ce_local, ("dp", "head"))
-    grad_rows = vocab_back(
-        head_rows, clipped, inside, embedding, n_col, log_total, mask_float / target_count
-    )
-    grad_final = col_sums(grad_rows)
+    ce_total = summed(jnp.sum(mask_float * (log_total - row_target)), ("dp", "head"))
+    coef = mask_float / target_count
+    target_coef = (coef * (jnp.exp(target_part - log_total) - 1.0)).astype(jnp.bfloat16)
+    target_coef = jnp.where(inside, target_coef.astype(jnp.float32), 0.0)
+    grad_rows = (
+        grad_rows * (coef * jnp.exp(base_part - log_total))[:, None]
+        + target_coef[:, None] * target_rows
+    )
+    grad_final = col_sums(grad_rows.astype(jnp.bfloat16)).astype(jnp.float32)
     grad_dec = norm_back(dec_three, norm_gain_rows[6], grad_final, head_scale)
     grad_dec = grad_dec + norm_back(
         dec_two, norm_gain_rows[5], ffn_backward(grad_dec, active_dec, units_dec), 1.0

time: 882 us -> 732 us (0.83)
  matrix products: 313 us -> 181 us
  waiting for transfers between devices: 217 us -> 174 us
  Pallas kernels: 0 us -> 35.9 us
    dot_general x8 -> x0, matrix products: 131 us -> none  [the longest x4 85.7 us: one_block(): return jnp.dot(grad_logits, embedding, preferred_element_type=jnp.float32)]
    pallas_call x0 -> x1, Pallas kernels: none -> 35.9 us  [head_pass(): pl.pallas_call(functools.partial(head_kernel, chunk, block), out_shape=(j...]
    reduce_scatter x3, waiting for transfers between devices: 104 us -> 79.5 us  [col_sums(): return lax.psum_scatter(terms, 'col', scatter_dimension=0, tiled=True)]
    gather x4 -> x1, local copies, waits for them, and re-layouts: 30.6 us -> 11 us  [per_device(): jnp.take(embedding, jnp.clip(local_t, 0, vocab_part - 1), axis=0)]
    reduce_sum x4 -> x1, other arithmetic: 18 us -> 2.29 us  [per_device(): jnp.sum(head_rows.astype(jnp.float32) * target_rows, axis=1)]
    squeeze x10 -> x11, local copies, waits for them, and re-layouts: 0.49 us -> 15.1 us  [per_device(): stats = merge_stats(stats, (others[0], others[1], others[2]))]
    all_gather x1, waiting for transfers between devices: 36.7 us -> 23.5 us  [col_rows(): return lax.all_gather(rows_low, 'col', axis=0, tiled=True)]
  transfers between devices with their start and end apart: 48 -> 48, of which waited for: 24 -> 23; matrix products, arithmetic and copies ran while one was open for 30% -> 39% of each run, Pallas kernels for 0% -> 0%
where the time goes in v2:
time: 732 us; the launch traced here: 721 us
  matrix products  181 us (25%)
  waiting for transfers between devices  174 us (24%)
  local copies, waits for them, and re-layouts  155 us (21%)
  starting transfers between devices  74.1 us (10%)
  other arithmetic  64.5 us (9%)
  Pallas kernels  35.9 us (5%)
  between operations  26.1 us (4%)
  blocking collectives  9.8 us (1%)
    dot_general x56, matrix products, contract(): lax.dot_general(left, right, (((left_dim,), (right_dim,)), ((), ())), pre...  93.9 us
    reduce_scatter x3, waiting for transfers between devices, col_sums(): return lax.psum_scatter(terms, 'col', scatter_dimension=0, tiled=True)  79.5 us
    ppermute x33, waiting for transfers between devices, swapped(): lax.ppermute(x, axis, [(i, i ^ step) for i in range(lax.axis_size(axis))])  38 us
    all_to_all x9, starting transfers between devices, head_trade(): lax.all_to_all(blocks, 'head', split_axis=0, concat_axis=0, tiled=True)  37 us
    ppermute x33, starting transfers between devices, swapped(): lax.ppermute(x, axis, [(i, i ^ step) for i in range(lax.axis_size(axis))])  36.7 us
    pallas_call x1, Pallas kernels, head_pass(): pl.pallas_call(functools.partial(head_kernel, chunk, block), out_shape=(j...  35.9 us
    all_to_all x9, waiting for transfers between devices, head_trade(): lax.all_to_all(blocks, 'head', split_axis=0, concat_axis=0, tiled=True)  33.3 us
    dot_general x12, matrix products, score_block(): jnp.einsum('qhd,khd->hqk', q_block, key_rows, preferred_element_type=jnp....  26.9 us
  transfers between devices with their start and end apart: 48, of which 23 were waited for; matrix products, arithmetic and copies ran while one was open for 39% of the time, Pallas kernels for 0%

profile of v2, /device:TPU:0, one launch (start us, length us, event | category | flops | bytes accessed | tf_op | source)
XLA Modules:
  0.0 720.6 jit_solution(16210828236911354707)
XLA Ops:
  8.9 3.1 collective-permute-start
  16.5 3.5 collective-permute-done.2
  21.0 10.6 %gather_fusion = bf16[1024,768]{1,0:T(8,128)(2,1)S(1)} fusion(bf16[8032,768]{1,0:T(8,128)(2,1)} %table_ref.1, s32[1024]{0:T(1024)S(1)} %get-tuple-element.1066), kind=kCustom, calls=%fused_computation.clone | custom fusion | bytes 3149824 | tf_op jit(solution)/shard_map/jit(_take)/gather | solution.py:524
  33.3 10.7 %gather_fusion.1 = bf16[1024,768]{1,0:T(8,128)(2,1)S(1)} fusion(bf16[8032,768]{1,0:T(8,128)(2,1)} %table_ref.1, s32[1024]{0:T(1024)S(1)} %get-tuple-element.1067), kind=kCustom, calls=%fused_computation.1.clone | custom fusion | bytes 3149824 | tf_op jit(solution)/shard_map/jit(_take)/gather | solution.py:524
  45.9 2.7 fusion.344
  52.8 15.0 %reduce-scatter.4.cloned.1.call-done = bf16[256,768]{1,0:T(8,128)(2,1)} async-done(((bf16[1024,768]{1,0:T(8,128)(2,1)}), bf16[256,768]{1,0:T(8,128)(2,1)}) %reduce-scatter.4.cloned.1.call-update) | async-done | bytes 393232 | tf_op jit(solution)/shard_map/reduce_scatter | solution.py:84
  78.8 3.7 all-to-all-start
  82.5 32.3 %reduce-scatter.6.cloned.1.call-done = bf16[256,768]{1,0:T(8,128)(2,1)} async-done(((bf16[1024,768]{1,0:T(8,128)(2,1)}), bf16[256,768]{1,0:T(8,128)(2,1)}) %reduce-scatter.6.cloned.1.call-update) | async-done | bytes 393232 | tf_op jit(solution)/shard_map/reduce_scatter | solution.py:84
  124.3 2.7 convolution_convert_fusion.4
  129.4 3.5 all-to-all-start.2
  143.9 18.2 %while.83 = (s32[]{:T(128)}, bf16[2,512,3,64]{1,3,2,0:T(8,128)(2,1)}, f32[2,3,512,1]{2,1,3,0:T(4,128)}, f32[2,3,512,1]{2,1,3,0:T(4,128)}, s32[2,512]{1,0:T(2,128...) while((s32[]{:T(128)}, ...), condition=%wide.region_7.9_spmd, body=%wide.region_4.8_spmd.sunk | while | flops 423196160 | bytes 22226052 | solution.py:121
  150.2 2.8 fusion.474
  159.3 2.8 fusion.474
  168.2 4.5 all-to-all-start.1
  176.6 11.6 %while.84 = (s32[]{:T(128)}, bf16[2,512,3,64]{1,3,2,0:T(8,128)(2,1)S(1)}, f32[2,3,512,1]{2,1,3,0:T(4,128)S(1)}, f32[2,3,512,1]{2,1,3,0:T(4,128)S(1)}, s32[2,512]...) while((s32[]{:T(128)}, ...), condition=%wide.region_16.18_spmd, body=%wide.region_13.17_spmd.sunk | while | flops 422147072 | bytes 22229108 | solution.py:121
  190.8 3.5 all-to-all-start.3
  199.7 3.0 all-to-all-done.3
  206.1 3.8 fusion.123
  210.0 5.9 multiply_reduce_fusion.10
  224.5 4.3 all-to-all-start.4
  229.1 15.7 %all-to-all-done.4 = bf16[4,3,256,192]{2,3,1,0:T(8,128)(2,1)} async-done(((bf16[4,3,256,192]{2,3,1,0:T(8,128)(2,1)}), bf16[4,3,256,192]{2,3,1,0:T(8,128)(2,1)}, u32[]{:S(2)}, u32[]{:S(2)}) %all-to-all-start.4) | async-done | bytes 1179680 | tf_op jit(solution)/shard_map/all_to_all | solution.py:88
  252.1 12.9 %while.85 = (s32[]{:T(128)}, bf16[2,512,3,64]{1,3,2,0:T(8,128)(2,1)}, f32[2,3,512,1]{2,1,3,0:T(4,128)S(1)}, f32[2,3,512,1]{2,1,3,0:T(4,128)S(1)}, s32[2,512]{1,0...) while((s32[]{:T(128)}, ...), condition=%wide.region_22.24_spmd, body=%wide.region_19.23_spmd.sunk | while | flops 422147072 | bytes 22225520 | solution.py:121
  255.7 2.9 fusion.484
  262.1 2.9 fusion.484
  268.5 9.8 %all_to_all.50 = bf16[4,256,192]{1,2,0:T(8,128)(2,1)S(1)} all-to-all(bf16[4,256,192]{1,2,0:T(8,128)(2,1)S(1)} %copy.318), channel_id=1, replica_groups=mesh['dp'=2,'head'=4,'col'=4] {'head'}, dimensions={0} | all-to-all | bytes 786432 | tf_op jit(solution)/shard_map/all_to_all | solution.py:88
  278.3 2.7 multiply_reduce_fusion.9
  281.6 4.1 fusion.115
  285.7 4.9 multiply_reduce_fusion.8
  293.2 11.0 %gather_fusion.2 = bf16[1024,768]{1,0:T(8,128)(2,1)S(1)} fusion(bf16[8032,768]{1,0:T(8,128)(2,1)} %table_ref.1, s32[1024]{0:T(1024)S(1)} %fusion.311), kind=kCustom, calls=%fused_computation.2.clone | custom fusion | bytes 3149824 | tf_op jit(solution)/shard_map/jit(_take)/gather | solution.py:581
  305.4 23.5 %all-gather.8.cloned.1.call-done.rows_ref = bf16[1024,768]{1,0:T(8,128)(2,1)} async-done(((bf16[256,768]{1,0:T(8,128)(2,1)}), bf16[1024,768]{1,0:T(8,128)(2,1)}) %all-gather.8.cloned.1.call-update) | async-done | bytes 1572880 | tf_op jit(solution)/shard_map/all_gather | solution.py:80
  329.0 35.9 %shard_map.234 = (f32[1024,768]{1,0:T(8,128)}, f32[1024,1]{1,0:T(8,128)}, f32[1024,1]{1,0:T(8,128)}) custom-call(bf16[1024,768]{1,0:T(8,128)(2,1)} %all-gather.8.cloned.1.call-done.rows_ref, s32[1024,1]{1,0:T(8,128)} %sub.268.target_ref, bf16[8032,768]{1,0:T(8,128)(2,1)} %table_ref.1), custom_call_target="tpu_custom_call" | custom-call | tf_op jit(solution)/shard_map/pallas_call | solution.py:454
  372.3 3.1 collective-permute-done.3
  404.5 2.8 collective-permute-start.10
  410.2 3.2 multiply_reduce_fusion.13
  418.1 32.2 %reduce-scatter.8.cloned.1.call-done = bf16[256,768]{1,0:T(8,128)(2,1)} async-done(((bf16[1024,768]{1,0:T(8,128)(2,1)}), bf16[256,768]{1,0:T(8,128)(2,1)}) %reduce-scatter.8.cloned.1.call-update) | async-done | bytes 393232 | tf_op jit(solution)/shard_map/reduce_scatter | solution.py:84
  452.3 9.0 %multiply_reduce_fusion.6 = (f32[256]{0:T(256)S(1)}, f32[256,768]{1,0:T(8,128)}) fusion(f32[256,768]{1,0:T(8,128)} %get-tuple-element.1051, f32[768]{0:T(1024)} %get-tuple-element.806, bf16[3072,1536]{1,0:T(8,128)(2,1)} %all-gather.6.cloned.1.call-done, f32[256,3072]{1,0:T(8,128)} %copy-done.133, f32[256,768]{1,0:T(8,128)} %copy-done.22, ...), kind=kOutput, calls=%fused_computation.321 | convolution fusion | flops 2420244224 | bytes 15344640 | tf_op jit(solution)/shard_map/dot_general | solution.py:185
  468.8 4.3 all-to-all-start.6
  476.7 4.1 collective-permute-done.18
  488.0 31.3 %while.86 = (s32[]{:T(128)}, f32[1024,3,64]{0,2,1:T(8,128)S(1)}, f32[1024,3,64]{0,2,1:T(8,128)}, bf16[2,512,3,64]{1,3,2,0:T(8,128)(2,1)}, bf16[2,512,3,64]{1,3,2...) while((s32[]{:T(128)}, f32[1024,3,64]{0,2,1:T(8,128)S(1)}, ...), condition=%wide.region_35.37_spmd.clone, body=%wide.region_33.36_spmd.clone.sunk | while | flops 1023965696 | bytes 123006320 | solution.py:180
  488.4 3.1 exponential_divide_fusion.6
  496.4 2.9 fusion.494
  503.5 3.1 exponential_divide_fusion.6
  511.5 2.9 fusion.494
  516.6 2.7 fusion.495
  526.7 4.4 all-to-all-start.7
  532.4 14.6 %all-to-all-done.7 = bf16[4,3,256,192]{2,3,1,0:T(8,128)(2,1)} async-done(((bf16[4,3,256,192]{2,3,1,0:T(8,128)(2,1)}), bf16[4,3,256,192]{2,3,1,0:T(8,128)(2,1)}, u32[]{:S(2)}, u32[]{:S(2)}) %all-to-all-start.7) | async-done | bytes 1179680 | tf_op jit(solution)/shard_map/all_to_all | solution.py:88
  555.4 4.2 all-to-all-start.9
  565.7 8.8 %multiply_reduce_fusion.4 = (f32[256]{0:T(256)S(1)}, f32[256,768]{1,0:T(8,128)}) fusion(f32[256,768]{1,0:T(8,128)} %copy-done.42, f32[768]{0:T(1024)S(1)} %copy-done.117, bf16[3072,1536]{1,0:T(8,128)(2,1)} %all-gather.4.cloned.1.call-done, f32[256,3072]{1,0:T(8,128)} %copy-done.132, f32[256,768]{1,0:T(8,128)S(1)} %copy-done.24, ...), kind=kOutput, calls=%fused_computation.319 | convolution fusion | flops 2419851008 | bytes 15734784 | tf_op jit(solution)/shard_map/dot_general | solution.py:185
  574.6 3.4 convolution_convert_fusion.1
  581.6 4.5 all-to-all-start.8
  588.6 27.5 %while.88 = (s32[]{:T(128)}, f32[1024,3,64]{0,2,1:T(8,128)S(1)}, bf16[2,512,3,64]{1,3,2,0:T(8,128)(2,1)}, bf16[2,512,3,64]{1,3,2,0:T(8,128)(2,1)S(1)}, s32[2,512...) while((s32[]{:T(128)}, f32[1024,3,64]{0,2,1:T(8,128)S(1)}, ...), condition=%wide.region_44.46_spmd.clone, body=%wide.region_42.45_spmd.clone.sunk | while | flops 823098368 | bytes 67763400 | solution.py:180
  591.2 3.1 exponential_divide_fusion.8
  598.8 3.5 fusion.512
  604.9 3.1 exponential_divide_fusion.8
  612.5 3.5 fusion.512
  622.7 23.2 %while.87 = (s32[]{:T(128)}, f32[1024,3,64]{0,2,1:T(8,128)S(1)}, bf16[2,512,3,64]{1,3,2,0:T(8,128)(2,1)}, bf16[2,512,3,64]{1,3,2,0:T(8,128)(2,1)S(1)}, s32[2,512...) while((s32[]{:T(128)}, f32[1024,3,64]{0,2,1:T(8,128)S(1)}, ...), condition=%wide.region_40.42_spmd.clone, body=%wide.region_38.41_spmd.clone.sunk | while | flops 822049280 | bytes 67759280 | solution.py:180
  623.1 3.1 exponential_divide_fusion.7
  630.7 3.5 fusion.503
  634.6 3.1 exponential_divide_fusion.7
  642.3 3.5 fusion.503
  666.3 3.5 collective-permute-done.29
  675.7 4.4 collective-permute-done.31
  692.1 4.1 collective-permute-start.7
  697.8 10.8 %collective-permute-done.27 = f32[8,8,768]{2,1,0:T(8,128)S(1)} collective-permute-done((f32[8,8,768]{2,1,0:T(8,128)S(1)}, f32[8,8,768]{2,1,0:T(8,128)S(1)}, u32[]{:S(2)}, u32[]{:S(2)}) %collective-permute-start.27) | collective-permute-done | bytes 196640 | tf_op jit(solution)/shard_map/ppermute | solution.py:29
  (711 shorter events, 299.4 us)
Async XLA Ops:
  8.0 674.2 %copy-start = (bf16[6,14,8,768]{3,2,1,0:T(8,128)(2,1)S(1)}, bf16[6,14,8,768]{3,2,1,0:T(8,128)(2,1)}, u32[]{:S(2)}) copy-start(bf16[6,14,8,768]{3,2,1,0:T(8,128)(2,1)} %param.44) | copy-start | bytes 3096580
  8.0 59.8 %reduce-scatter.4.cloned.1.call-start = ((), (), s32[]{:S(2)}) async-start(), calls=%async_computation.13 | async-start | bytes 1966080 | tf_op jit(solution)/shard_map/reduce_scatter | solution.py:84
  8.9 5.6 collective-permute-start
  11.9 4.5 collective-permute-start.1
  14.5 5.4 collective-permute-start.2
  33.3 81.6 %reduce-scatter.6.cloned.1.call-start = ((), (), s32[]{:S(2)}) async-start(), calls=%async_computation.14 | async-start | bytes 1966080 | tf_op jit(solution)/shard_map/reduce_scatter | solution.py:84
  45.8 160.4 %all-gather.4.cloned.1.call-start = ((), (), s32[]{:S(2)}) async-start(), calls=%async_computation.15 | async-start | bytes 9732096 | tf_op jit(solution)/shard_map/all_gather | solution.py:338
  49.4 231.6 %all-gather.6.cloned.1.call-start = ((), (), s32[]{:S(2)}) async-start(), calls=%async_computation.16 | async-start | bytes 9732096 | tf_op jit(solution)/shard_map/all_gather | solution.py:338
  51.5 165.5 %copy-start.63 = (bf16[6,8,768]{2,1,0:T(8,128)(2,1)}, bf16[6,8,768]{2,1,0:T(8,128)(2,1)S(1)}, u32[]{:S(2)}) copy-start(bf16[6,8,768]{2,1,0:T(8,128)(2,1)S(1)} %convert_element_type.261) | copy-start | bytes 221188
  77.5 38.6 %copy-start.114 = (f32[768]{0:T(1024)S(1)}, f32[768]{0:T(1024)}, u32[]{:S(2)}) copy-start(f32[768]{0:T(1024)} %get-tuple-element.803) | copy-start | bytes 9220
  78.8 50.7 %all-to-all-start = ((bf16[4,3,256,192]{2,3,1,0:T(8,128)(2,1)}), bf16[4,3,256,192]{2,3,1,0:T(8,128)(2,1)S(1)}, u32[]{:S(2)}, u32[]{:S(2)}) async-start(bf16[4,3,256,192]{2,3,1,0:T(8,128)(2,1)} %copy.292), calls=%async_computation.1 | async-start | bytes 2359296 | tf_op jit(solution)/shard_map/all_to_all | solution.py:88
  129.4 38.8 %all-to-all-start.2 = ((bf16[4,3,256,192]{2,3,1,0:T(8,128)(2,1)}), bf16[4,3,256,192]{2,3,1,0:T(8,128)(2,1)S(1)}, u32[]{:S(2)}, u32[]{:S(2)}) async-start(bf16[4,3,256,192]{2,3,1,0:T(8,128)(2,1)} %copy.303), calls=%async_computation.4 | async-start | bytes 2359296 | tf_op jit(solution)/shard_map/all_to_all | solution.py:88
  168.2 22.6 %all-to-all-start.1 = ((bf16[4,256,192]{1,2,0:T(8,128)(2,1)}), bf16[4,256,192]{1,2,0:T(8,128)(2,1)}, u32[]{:S(2)}, u32[]{:S(2)}) async-start(bf16[4,256,192]{1,2,0:T(8,128)(2,1)} %copy.298), calls=%async_computation.2 | async-start | bytes 786432 | tf_op jit(solution)/shard_map/all_to_all | solution.py:88
  190.8 11.9 %all-to-all-start.3 = ((bf16[4,256,192]{1,2,0:T(8,128)(2,1)}), bf16[4,256,192]{1,2,0:T(8,128)(2,1)S(1)}, u32[]{:S(2)}, u32[]{:S(2)}) async-start(bf16[4,256,192]{1,2,0:T(8,128)(2,1)} %copy.309), calls=%async_computation.5 | async-start | bytes 786432 | tf_op jit(solution)/shard_map/all_to_all | solution.py:88
  196.3 82.0 %copy-start.18 = (f32[256,768]{1,0:T(8,128)}, f32[256,768]{1,0:T(8,128)S(1)}, u32[]{:S(2)}) copy-start(f32[256,768]{1,0:T(8,128)S(1)} %get-tuple-element.1049) | copy-start | bytes 2359300
  224.5 20.2 %all-to-all-start.4 = ((bf16[4,3,256,192]{2,3,1,0:T(8,128)(2,1)}), bf16[4,3,256,192]{2,3,1,0:T(8,128)(2,1)}, u32[]{:S(2)}, u32[]{:S(2)}) async-start(bf16[4,3,256,192]{2,3,1,0:T(8,128)(2,1)} %copy.312), calls=%async_computation.6 | async-start | bytes 2359296 | tf_op jit(solution)/shard_map/all_to_all | solution.py:88
  228.8 100.1 %all-gather.8.cloned.1.call-start = ((), (), s32[]{:S(2)}) async-start(), calls=%async_computation.17 | async-start | bytes 1966080 | tf_op jit(solution)/shard_map/all_gather | solution.py:80
  291.8 158.5 %reduce-scatter.8.cloned.1.call-start = ((), (), s32[]{:S(2)}) async-start(), calls=%async_computation.18 | async-start | bytes 1966080 | tf_op jit(solution)/shard_map/reduce_scatter | solution.py:84
  364.9 31.2 %copy-start.62 = (s32[4,4,4,64]{3,2,1,0:T(4,128)S(1)}, s32[4,4,4,64]{3,2,1,0:T(4,128)}, u32[]{:S(2)}) copy-start(s32[4,4,4,64]{3,2,1,0:T(4,128)} %copy-done.61) | copy-start | bytes 49156
  371.7 3.8 collective-permute-start.3
  378.0 12.5 %collective-permute-start.4 = (f32[3,1024]{1,0:T(4,128)}, f32[3,1024]{1,0:T(4,128)}, u32[]{:S(2)}, u32[]{:S(2)}) collective-permute-start(f32[3,1024]{1,0:T(4,128)} %pad_maximum_fusion.12), channel_id=1, source_target_pairs={{0,2},{1,3},{2,0},{3,1},{4,6},{5,7},{6,4},{7,5},{8,10},{9,11},{10,... | collective-permute-start | bytes 36872 | tf_op jit(solution)/shard_map/ppermute | solution.py:29
  397.5 3.8 collective-permute-start.8
  402.6 1.4 collective-permute-start.9
  404.5 3.7 collective-permute-start.10
  413.5 38.8 %copy-start.105 = (f32[256]{0:T(256)S(1)}, f32[256]{0:T(256)}, u32[]{:S(2)}) copy-start(f32[256]{0:T(256)} %copy-done.104) | copy-start | bytes 3076
  416.1 59.2 %collective-permute-start.20 = (bf16[16,256]{1,0:T(8,128)(2,1)S(1)}, bf16[16,256]{1,0:T(8,128)(2,1)S(1)}, u32[]{:S(2)}, u32[]{:S(2)}) collective-permute-start(bf16[16,256]{1,0:T(8,128)(2,1)S(1)} %get-tuple-element.1041), channel_id=1, source_target_pairs={{0,4},{4,0},{8,12},{12,8},{1,5},{5,1},{9,13},{13,9},{2,6},{6,2},{1... | collective-permute-start | bytes 24584 | tf_op jit(solution)/shard_map/ppermute | solution.py:29
  416.2 59.2 %collective-permute-start.21 = (bf16[16,256]{1,0:T(8,128)(2,1)S(1)}, bf16[16,256]{1,0:T(8,128)(2,1)}, u32[]{:S(2)}, u32[]{:S(2)}) collective-permute-start(bf16[16,256]{1,0:T(8,128)(2,1)S(1)} %get-tuple-element.1041), channel_id=1, source_target_pairs={{0,8},{4,12},{8,0},{12,4},{1,9},{5,13},{9,1},{13,5},{2,10},{6,14},... | collective-permute-start | bytes 24584 | tf_op jit(solution)/shard_map/ppermute | solution.py:29
  417.7 57.7 %collective-permute-start.22 = (bf16[16,256]{1,0:T(8,128)(2,1)S(1)}, bf16[16,256]{1,0:T(8,128)(2,1)}, u32[]{:S(2)}, u32[]{:S(2)}) collective-permute-start(bf16[16,256]{1,0:T(8,128)(2,1)S(1)} %get-tuple-element.1041), channel_id=1, source_target_pairs={{0,12},{4,8},{8,4},{12,0},{1,13},{5,9},{9,5},{13,1},{2,14},{6,10},... | collective-permute-start | bytes 24584 | tf_op jit(solution)/shard_map/ppermute | solution.py:29
  468.8 12.6 %all-to-all-start.6 = ((bf16[4,256,192]{1,2,0:T(8,128)(2,1)}), bf16[4,256,192]{1,2,0:T(8,128)(2,1)}, u32[]{:S(2)}, u32[]{:S(2)}) async-start(bf16[4,256,192]{1,2,0:T(8,128)(2,1)} %bitcast.712), calls=%async_computation.9 | async-start | bytes 786432 | tf_op jit(solution)/shard_map/all_to_all | solution.py:88
  473.2 3.5 collective-permute-start.17
  473.7 7.1 collective-permute-start.18
  475.4 5.4 collective-permute-start.19
  526.7 24.5 %copy-start.28 = (bf16[256,768]{1,0:T(8,128)(2,1)S(1)}, bf16[256,768]{1,0:T(8,128)(2,1)}, u32[]{:S(2)}) copy-start(bf16[256,768]{1,0:T(8,128)(2,1)} %copy-done.27) | copy-start | bytes 1179652
  526.7 20.3 %all-to-all-start.7 = ((bf16[4,3,256,192]{2,3,1,0:T(8,128)(2,1)}), bf16[4,3,256,192]{2,3,1,0:T(8,128)(2,1)}, u32[]{:S(2)}, u32[]{:S(2)}) async-start(bf16[4,3,256,192]{2,3,1,0:T(8,128)(2,1)} %copy.336), calls=%async_computation.10 | async-start | bytes 2359296 | tf_op jit(solution)/shard_map/all_to_all | solution.py:88
  551.4 29.1 %copy-start.47 = (f32[1,8,768]{2,1,0:T(8,128)}, f32[1,8,768]{2,1,0:T(8,128)S(1)}, u32[]{:S(2)}) copy-start(f32[1,8,768]{2,1,0:T(8,128)S(1)} %convolution_bitcast_fusion.2) | copy-start | bytes 73732
  555.4 26.3 %all-to-all-start.9 = ((bf16[4,256,192]{1,2,0:T(8,128)(2,1)}), bf16[4,256,192]{1,2,0:T(8,128)(2,1)}, u32[]{:S(2)}, u32[]{:S(2)}) async-start(bf16[4,256,192]{1,2,0:T(8,128)(2,1)} %bitcast.711), calls=%async_computation.12 | async-start | bytes 786432 | tf_op jit(solution)/shard_map/all_to_all | solution.py:88
  581.2 82.0 %collective-permute-start.28 = (f32[4,8,768]{2,1,0:T(8,128)}, f32[4,8,768]{2,1,0:T(8,128)}, u32[]{:S(2)}, u32[]{:S(2)}) collective-permute-start(f32[4,8,768]{2,1,0:T(8,128)} %pad_maximum_fusion.6), channel_id=1, source_target_pairs={{0,4},{4,0},{8,12},{12,8},{1,5},{5,1},{9,13},{13,9},{2,6},{6,2},{1... | collective-permute-start | bytes 294920 | tf_op jit(solution)/shard_map/ppermute | solution.py:29
  581.6 36.8 %all-to-all-start.8 = ((bf16[4,256,192]{1,2,0:T(8,128)(2,1)}), bf16[4,256,192]{1,2,0:T(8,128)(2,1)}, u32[]{:S(2)}, u32[]{:S(2)}) async-start(bf16[4,256,192]{1,2,0:T(8,128)(2,1)} %bitcast.116), calls=%async_computation.11 | async-start | bytes 786432 | tf_op jit(solution)/shard_map/all_to_all | solution.py:88
  622.6 24.8 %copy-start.79 = (bf16[8,4,256]{2,0,1:T(8,128)(2,1)S(1)}, bf16[8,4,256]{2,0,1:T(8,128)(2,1)}, u32[]{:S(2)}) copy-start(bf16[8,4,256]{2,0,1:T(8,128)(2,1)} %get-tuple-element.1006) | copy-start | bytes 49156
  622.6 26.1 %copy-start.78 = (bf16[8,4,256]{2,0,1:T(8,128)(2,1)S(1)}, bf16[8,4,256]{2,0,1:T(8,128)(2,1)}, u32[]{:S(2)}) copy-start(bf16[8,4,256]{2,0,1:T(8,128)(2,1)} %get-tuple-element.1007) | copy-start | bytes 49156
  653.2 29.0 %copy-start.41 = (f32[6,8,768]{2,1,0:T(8,128)S(1)}, f32[6,8,768]{2,1,0:T(8,128)}, u32[]{:S(2)}) copy-start(f32[6,8,768]{2,1,0:T(8,128)} %param.45) | copy-start | bytes 442372
  653.3 4.2 collective-permute-start.11
  653.8 5.3 collective-permute-start.12
  655.4 3.7 collective-permute-start.13
  655.6 6.1 collective-permute-start.14
  657.5 4.2 collective-permute-start.15
  659.1 3.2 collective-permute-start.16
  663.0 45.7 %copy-start.46 = (f32[6,8,768]{2,1,0:T(8,128)S(1)}, f32[6,8,768]{2,1,0:T(8,128)}, u32[]{:S(2)}) copy-start(f32[6,8,768]{2,1,0:T(8,128)} %param.46) | copy-start | bytes 442372
  663.0 45.7 %copy-start.68 = (f32[6,8,768]{2,1,0:T(8,128)S(1)}, f32[6,8,768]{2,1,0:T(8,128)}, u32[]{:S(2)}) copy-start(f32[6,8,768]{2,1,0:T(8,128)} %param.50) | copy-start | bytes 442372
  663.0 45.7 %copy-start.69 = (f32[6,8,768]{2,1,0:T(8,128)S(1)}, f32[6,8,768]{2,1,0:T(8,128)}, u32[]{:S(2)}) copy-start(f32[6,8,768]{2,1,0:T(8,128)} %param.49) | copy-start | bytes 442372
  663.0 2.6 collective-permute-start.23
  664.1 5.7 collective-permute-start.29
  665.6 45.2 %copy-start.70 = (f32[6,8,768]{2,1,0:T(8,128)S(1)}, f32[6,8,768]{2,1,0:T(8,128)}, u32[]{:S(2)}) copy-start(f32[6,8,768]{2,1,0:T(8,128)} %param.48) | copy-start | bytes 442372
  665.6 45.2 %copy-start.71 = (f32[6,8,768]{2,1,0:T(8,128)S(1)}, f32[6,8,768]{2,1,0:T(8,128)}, u32[]{:S(2)}) copy-start(f32[6,8,768]{2,1,0:T(8,128)} %param.47) | copy-start | bytes 442372
  665.7 7.9 %collective-permute-start.24 = (f32[8,8,768]{2,1,0:T(8,128)S(1)}, f32[8,8,768]{2,1,0:T(8,128)S(1)}, u32[]{:S(2)}, u32[]{:S(2)}) collective-permute-start(f32[8,8,768]{2,1,0:T(8,128)S(1)} %add.467), channel_id=1, source_target_pairs={{0,8},{4,12},{8,0},{12,4},{1,9},{5,13},{9,1},{13,5},{2,10},{6,14},... | collective-permute-start | bytes 589832 | tf_op jit(solution)/shard_map/ppermute | solution.py:29
  670.8 4.7 collective-permute-start.30
  673.5 8.0 %collective-permute-start.25 = (f32[8,8,768]{2,1,0:T(8,128)S(1)}, f32[8,8,768]{2,1,0:T(8,128)S(1)}, u32[]{:S(2)}, u32[]{:S(2)}) collective-permute-start(f32[8,8,768]{2,1,0:T(8,128)S(1)} %add.468), channel_id=1, source_target_pairs={{0,16},{16,0},{1,17},{17,1},{2,18},{18,2},{3,19},{19,3},{4,20},{20... | collective-permute-start | bytes 589832 | tf_op jit(solution)/shard_map/ppermute | solution.py:29
  675.5 4.7 collective-permute-start.31
  680.2 16.9 %collective-permute-start.32 = (f32[4,8,768]{2,1,0:T(8,128)S(1)}, f32[4,8,768]{2,1,0:T(8,128)S(1)}, u32[]{:S(2)}, u32[]{:S(2)}) collective-permute-start(f32[4,8,768]{2,1,0:T(8,128)S(1)} %add.475), channel_id=1, source_target_pairs={{0,2},{1,3},{2,0},{3,1},{4,6},{5,7},{6,4},{7,5},{8,10},{9,11},{10,... | collective-permute-start | bytes 294920 | tf_op jit(solution)/shard_map/ppermute | solution.py:29
  681.6 15.6 %collective-permute-start.26 = (f32[8,8,768]{2,1,0:T(8,128)S(1)}, f32[8,8,768]{2,1,0:T(8,128)S(1)}, u32[]{:S(2)}, u32[]{:S(2)}) collective-permute-start(f32[8,8,768]{2,1,0:T(8,128)S(1)} %add.469), channel_id=1, source_target_pairs={{0,1},{1,0},{2,3},{3,2},{4,5},{5,4},{6,7},{7,6},{8,9},{9,8},{10,11... | collective-permute-start | bytes 589832 | tf_op jit(solution)/shard_map/ppermute | solution.py:29
  685.1 3.8 collective-permute-start.5
  690.2 1.2 collective-permute-start.6
  692.1 4.3 collective-permute-start.7
  697.2 11.5 %collective-permute-start.27 = (f32[8,8,768]{2,1,0:T(8,128)S(1)}, f32[8,8,768]{2,1,0:T(8,128)S(1)}, u32[]{:S(2)}, u32[]{:S(2)}) collective-permute-start(f32[8,8,768]{2,1,0:T(8,128)S(1)} %add.470), channel_id=1, source_target_pairs={{0,2},{1,3},{2,0},{3,1},{4,6},{5,7},{6,4},{7,5},{8,10},{9,11},{10,... | collective-permute-start | bytes 589832 | tf_op jit(solution)/shard_map/ppermute | solution.py:29
  (128 other events, 881.2 us)
Sparse Core Ops, SparseCore 0:
  33.4 34.3 reduce-scatter.3
  70.1 44.6 reduce-scatter.5
  291.9 37.0 all-gather.7
  415.5 34.6 reduce-scatter.7
Sparse Core Ops, SparseCore 1:
  49.5 109.7 all-gather.3
  162.0 82.3 all-gather.5
